TPU v7x, 32 devices: a whole 2x2x4 slice. The times are simulated.
32 devices in a mesh: cell: 8 (over y, x, core), img: 4 (over z).
Axes of the slice: x: 2, y: 2, z: 4, core: 2. Of those that a mesh axis runs over, the one named last changes fastest.
Arguments:
- jac_cam: float32 [18, 262144], P(None, ('cell', 'img')), may hold values from -0.75 to 0.75
- jac_pt: float32 [6, 262144], P(None, ('cell', 'img')), may hold values from -6 to 6
- obs_residual: float32 [2, 262144], P(None, ('cell', 'img')), may hold values from -6 to 6
- obs_point: int32 [262144], P(('cell', 'img')), may hold values from 0 to 1023
- obs_slot: int32 [262144], P(('cell', 'img')), may hold values from 0 to 2047
- request: int32 [1024, 64], P(('cell', 'img')), may hold values from 0 to 767, as said below
- obs_count: int32 [32], P(('cell', 'img')), may hold values from 4096 to 8192, as said below
- cam_damp: float32 [9, 24576], P(None, ('cell', 'img')), may hold values from 0.16 to 2
- pt_damp: float32 [32768], P(('cell', 'img')), may hold values from 1 to 8
Outputs:
- camera_update: float32 [9, 24576], P(None, ('cell', 'img'))
- camera_residual: float32 [9, 24576], P(None, ('cell', 'img'))
Inputs may be any that keep to these rules, and one draw needn't show every extreme that they name: obs_point indexes the observation's device's block of 1024 points. `obs_slot`: slot s of a device names column s % 64 of its request row s // 64. `request`: row w of a device's 32 rows lists 64 different cameras of owner device w, as indices within that owner's 768 cameras. `obs_count`: some device has all 8192 slots live.
All inputs are finite; a program needn't handle non-finite values.
Results may differ from a plain program's by a relative error of at most 0.00016.
Values sent between devices are 32-bit elements; how exact they have to be, the bound alone decides.
No kernel may reach another device: no remote copies, remote signals or barrier semaphores. Data moves between devices by JAX's collectives and lax.ppermute only.
A program may use at most 128 MiB of HBM per device.

v0:
```python
import functools

import jax
import jax.numpy as jnp
from jax import lax
from jax.experimental import pallas as pl
from jax.experimental.pallas import tpu as pltpu
from jax.sharding import PartitionSpec as P

AXES = ("cell", "img")
F32 = jnp.float32
BF16 = jnp.bfloat16
LANES = 128
CAP = 64
VMEM_BYTES = 48 * 1024 * 1024


def iota(shape, dim):
    return lax.broadcasted_iota(jnp.int32, shape, dim)


def take_lanes(table, lanes):
    return jnp.take_along_axis(table, lanes, axis=1, mode="promise_in_bounds")


def contract(left, right):
    return lax.dot_general(left, right, (((1,), (1,)), ((), ())), preferred_element_type=F32)


def one_hot_rows(index, rows):
    hit = iota((rows, index.shape[1]), 0) == index
    return jnp.where(hit, 1.0, 0.0).astype(BF16)


def rounded_parts(value, count):
    parts = []
    for _ in range(count):
        part = value.astype(BF16)
        parts.append(part)
        value = value - part.astype(F32)
    return parts


def spread_groups(tiles, group, groups):
    rows = []
    width = group.shape[1]
    for number in range(groups):
        hit = jnp.where(jnp.broadcast_to(group, (16, width)) == number, 1.0, 0.0).astype(BF16)
        rows += [tile * hit for tile in tiles]
    return jnp.concatenate(rows, axis=0)


def swap_halves(value):
    return pltpu.roll(value, CAP, 1)


def unpack_pair(even, odd):
    left = iota((8, LANES), 1) < CAP
    return jnp.where(left, even, swap_halves(odd)), jnp.where(left, swap_halves(even), odd)


def pack_pair(low, high):
    left = iota((8, LANES), 1) < CAP
    return jnp.where(left, low, swap_halves(high)), jnp.where(left, swap_halves(low), high)


def scalar_spot():
    return (iota((8, LANES), 0) == 1) & (iota((8, LANES), 1) >= CAP)


def sum_all(value):
    return jnp.sum(jnp.sum(value, axis=1, keepdims=True), axis=0, keepdims=True)


def carried_scalar(ref):
    total = ref[0]
    for sender in range(1, ref.shape[0]):
        total = total + ref[sender]
    return total[1:2, CAP:CAP + 1]


def store_pairs(out_ref, sums_ref, rows_each, offset, top, scalar):
    width = sums_ref.shape[1]
    for group in range(sums_ref.shape[0] // rows_each):
        start = group * rows_each + offset
        block = sums_ref[start:start + 16, :] + sums_ref[start + 16:start + 32, :]
        for part in range(width // LANES):
            pair = group * (width // LANES) + part
            lanes = slice(part * LANES, (part + 1) * LANES)
            even, odd = pack_pair(block[0:8, lanes], block[8:16, lanes])
            if scalar is not None:
                even = jnp.where(scalar_spot(), scalar, even)
                odd = jnp.where(scalar_spot(), scalar, odd)
            out_ref[2 * pair, top:top + 8] = even
            out_ref[2 * pair + 1, top:top + 8] = odd


def point_spread(solved_ref, point, jac_a, jac_b):
    low = jnp.broadcast_to(point & (LANES - 1), (8, LANES))
    hit = jnp.broadcast_to(point >> 7, (8, LANES)) == iota((8, LANES), 0)
    first = jnp.zeros((8, LANES), F32)
    second = jnp.zeros((8, LANES), F32)
    for axis in range(3):
        taken = jnp.where(hit, take_lanes(solved_ref[axis], low), 0.0)
        first = first + jac_a[axis:axis + 1] * taken
        second = second + jac_b[axis:axis + 1] * taken
    return jnp.sum(first, axis=0, keepdims=True), jnp.sum(second, axis=0, keepdims=True)


def live_group(index, shift, start, count):
    spot = iota(index.shape, 1) + start
    return jnp.where(spot < count, index >> shift, -1)


def solve_points(inverse_ref, totals, solved_ref):
    rows = ((0, 3, 5), (3, 1, 4), (5, 4, 2))
    for axis in range(3):
        solved_ref[axis] = (
            inverse_ref[rows[axis][0]] * totals[0]
            + inverse_ref[rows[axis][1]] * totals[1]
            + inverse_ref[rows[axis][2]] * totals[2]
        )


def start_kernel(chunk, count_ref, cam_ref, pt_ref, err_ref, point_ref, slot_ref, req_ref, damp_ref,
                 out_ref, camp_ref, pta_ref, ptb_ref, inverse_ref, psum_ref, ssum_ref, solved_ref):
    nobs = cam_ref.shape[1]
    count = count_ref[0]
    psum_ref[...] = jnp.zeros_like(psum_ref)
    ssum_ref[...] = jnp.zeros_like(ssum_ref)
    groups = ssum_ref.shape[0] // 64

    def gather_points(step, carry):
        start = pl.multiple_of(step * chunk, chunk)
        lanes = pl.ds(start, chunk)
        point = point_ref[:, lanes]
        jac = pt_ref[:, lanes]
        zero = jnp.zeros((1, chunk), F32)
        jac_a = jnp.concatenate([jac[0:3], zero, jac[0:3], zero], axis=0)
        jac_b = jnp.concatenate([jac[3:6], zero, jac[3:6], zero], axis=0)
        pta_ref[:, lanes] = jac_a
        ptb_ref[:, lanes] = jac_b
        turn_a = jnp.concatenate([jac[0:3], zero, jac[1:3], jac[0:1], zero], axis=0)
        turn_b = jnp.concatenate([jac[3:6], zero, jac[4:6], jac[3:4], zero], axis=0)
        err = err_ref[:, lanes]
        blocks = jac_a * turn_a + jac_b * turn_b
        sides = jac_a * err[0:1] + jac_b * err[1:2]
        tiles = rounded_parts(jnp.concatenate([blocks, sides], axis=0), 3)
        spread = spread_groups(tiles, live_group(point, 7, start, count), 8)
        psum_ref[...] += contract(spread, one_hot_rows(point & (LANES - 1), LANES))
        return carry

    lax.fori_loop(0, nobs // chunk, gather_points, 0)

    def row(number):
        total = psum_ref[pl.ds(number, 8, stride=48), :]
        total = total + psum_ref[pl.ds(number + 16, 8, stride=48), :]
        return total + psum_ref[pl.ds(number + 32, 8, stride=48), :]

    damp = damp_ref[...]
    m00, m11, m22 = row(0) + damp, row(1) + damp, row(2) + damp
    m01, m12, m20 = row(4), row(5), row(6)
    c00 = m11 * m22 - m12 * m12
    c01 = m12 * m20 - m01 * m22
    c02 = m01 * m12 - m11 * m20
    c11 = m22 * m00 - m20 * m20
    c12 = m20 * m01 - m12 * m00
    c22 = m00 * m11 - m01 * m01
    det = m00 * c00 + m01 * c01 + m20 * c02
    for place, cofactor in enumerate((c00, c11, c22, c01, c12, c02)):
        inverse_ref[place] = cofactor / det
    solve_points(inverse_ref, [row(8), row(9), row(10)], solved_ref)

    def scatter_terms(step, carry):
        start = pl.multiple_of(step * chunk, chunk)
        lanes = pl.ds(start, chunk)
        slot = slot_ref[:, lanes]
        camp_ref[0:9, lanes] = cam_ref[0:9, lanes]
        camp_ref[9:16, lanes] = jnp.zeros((7, chunk), F32)
        camp_ref[16:25, lanes] = cam_ref[9:18, lanes]
        camp_ref[25:32, lanes] = jnp.zeros((7, chunk), F32)
        kept_a, kept_b = [], []
        for tile in range(chunk // LANES):
            spot = pl.ds(start + tile * LANES, LANES)
            first, second = point_spread(solved_ref, point_ref[:, spot], pta_ref[:, spot], ptb_ref[:, spot])
            err = err_ref[:, spot]
            kept_a.append(err[0:1] - first)
            kept_b.append(err[1:2] - second)
        kept_a = jnp.concatenate(kept_a, axis=1)
        kept_b = jnp.concatenate(kept_b, axis=1)
        cam_a = camp_ref[0:16, lanes]
        cam_b = camp_ref[16:32, lanes]
        rhs = -(cam_a * kept_a + cam_b * kept_b)
        diag = cam_a * cam_a + cam_b * cam_b
        tiles = rounded_parts(rhs, 2) + rounded_parts(diag, 2)
        spread = spread_groups(tiles, live_group(slot, 8, start, count), groups)
        ssum_ref[...] += contract(spread, one_hot_rows(slot & 255, 256))
        return carry

    lax.fori_loop(0, nobs // chunk, scatter_terms, 0)
    store_pairs(out_ref, ssum_ref, 64, 0, 0, None)
    store_pairs(out_ref, ssum_ref, 64, 32, 8, None)
    wanted = req_ref[...].astype(F32)
    wanted = jnp.concatenate([jnp.zeros_like(wanted), wanted], axis=1)
    for owner in range(req_ref.shape[0]):
        out_ref[owner, 8:16] = jnp.where(scalar_spot(), wanted[owner:owner + 1], out_ref[owner, 8:16])


def apply_kernel(chunk, first, *refs):
    if first:
        (count_ref, in_ref, camp_ref, pta_ref, ptb_ref, point_ref, slot_ref, inverse_ref, damp_ref, precond_ref,
         out_ref, table_ref, rz_ref, psum_ref, ssum_ref, solved_ref, along_ref, last_ref) = refs
    else:
        (count_ref, in_ref, camp_ref, pta_ref, ptb_ref, point_ref, slot_ref, inverse_ref, damp_ref, precond_ref,
         oldtable_ref, oldrz_ref, oldown_ref,
         out_ref, own_ref, rz_ref, psum_ref, ssum_ref, solved_ref, along_ref, last_ref, table_ref) = refs
    nobs = camp_ref.shape[1]
    count = count_ref[0]
    psum_ref[...] = jnp.zeros_like(psum_ref)
    ssum_ref[...] = jnp.zeros_like(ssum_ref)
    groups = ssum_ref.shape[0] // 32
    pairs = in_ref.shape[0] // 2
    rz = carried_scalar(in_ref)
    rz_ref[...] = jnp.broadcast_to(rz, rz_ref.shape)
    own = precond_ref[...]
    if not first:
        beta = rz / oldrz_ref[0:1, 0:1]
        own = own + beta * oldown_ref[...]
        own_ref[...] = own
    for pair in range(pairs):
        low, high = unpack_pair(in_ref[2 * pair], in_ref[2 * pair + 1])
        if not first:
            low = low + beta * oldtable_ref[pair, 0:8]
            high = high + beta * oldtable_ref[pair, 8:16]
        table_ref[pair, 0:8] = low
        table_ref[pair, 8:16] = high
        last_ref[pair:pair + 1, :] = high[0:1]

    def gather_points(step, carry):
        start = pl.multiple_of(step * chunk, chunk)
        lanes = pl.ds(start, chunk)
        for tile in range(chunk // LANES):
            spot = pl.ds(start + tile * LANES, LANES)
            slot = slot_ref[:, spot]
            low = jnp.broadcast_to(slot & (LANES - 1), (8, LANES))
            high = jnp.broadcast_to(slot >> 7, (8, LANES))
            taken = jnp.zeros((8, LANES), F32)
            for pair in range(pairs):
                taken = jnp.where(high == pair, take_lanes(table_ref[pair, 0:8], low), taken)
            tail = jnp.zeros((8, LANES), F32)
            for base in range(0, pairs, 8):
                hit = high == iota((8, LANES), 0) + base
                tail = jnp.where(hit, take_lanes(last_ref[base:base + 8], low), tail)
            tail = jnp.sum(tail, axis=0, keepdims=True)
            along_ref[0:1, spot] = jnp.sum(camp_ref[0:8, spot] * taken, axis=0, keepdims=True) + camp_ref[8:9, spot] * tail
            along_ref[1:2, spot] = jnp.sum(camp_ref[16:24, spot] * taken, axis=0, keepdims=True) + camp_ref[24:25, spot] * tail
        point = point_ref[:, lanes]
        sides = pta_ref[:, lanes] * along_ref[0:1, lanes] + ptb_ref[:, lanes] * along_ref[1:2, lanes]
        parts = rounded_parts(sides, 3)
        later = jnp.where(iota((8, chunk), 0) < 4, parts[1].astype(F32), parts[2].astype(F32))
        tile = jnp.concatenate([parts[0].astype(F32), later], axis=0).astype(BF16)
        spread = spread_groups([tile], live_group(point, 7, start, count), 8)
        psum_ref[...] += contract(spread, one_hot_rows(point & (LANES - 1), LANES))
        return carry

    lax.fori_loop(0, nobs // chunk, gather_points, 0)

    def row(number):
        total = psum_ref[pl.ds(number, 8, stride=16), :]
        total = total + psum_ref[pl.ds(number + 8, 8, stride=16), :]
        return total + psum_ref[pl.ds(number + 12, 8, stride=16), :]

    solve_points(inverse_ref, [row(0), row(1), row(2)], solved_ref)

    def scatter_terms(step, carry):
        start = pl.multiple_of(step * chunk, chunk)
        lanes = pl.ds(start, chunk)
        slot = slot_ref[:, lanes]
        kept_a, kept_b = [], []
        for tile in range(chunk // LANES):
            spot = pl.ds(start + tile * LANES, LANES)
            first_sum, second_sum = point_spread(solved_ref, point_ref[:, spot], pta_ref[:, spot], ptb_ref[:, spot])
            kept_a.append(along_ref[0:1, spot] - first_sum)
            kept_b.append(along_ref[1:2, spot] - second_sum)
        kept_a = jnp.concatenate(kept_a, axis=1)
        kept_b = jnp.concatenate(kept_b, axis=1)
        terms = camp_ref[0:16, lanes] * kept_a + camp_ref[16:32, lanes] * kept_b
        spread = spread_groups(rounded_parts(terms, 2), live_group(slot, 8, start, count), groups)
        ssum_ref[...] += contract(spread, one_hot_rows(slot & 255, 256))
        energy = along_ref[0:1, lanes] * kept_a + along_ref[1:2, lanes] * kept_b
        energy = jnp.where(iota((1, chunk), 1) + start < count, energy, 0.0)
        return carry + energy

    energy = lax.fori_loop(0, nobs // chunk, scatter_terms, jnp.zeros((1, chunk), F32))
    partial = sum_all(energy) + sum_all(damp_ref[...] * own * own)
    store_pairs(out_ref, ssum_ref, 32, 0, 0, partial)


def owner_sums(values, ids, cameras):
    groups = cameras // 256
    tiles = []
    for value in values:
        tiles += rounded_parts(value, 2)
    spread = spread_groups(tiles, ids >> 8, groups)
    sums = contract(spread, one_hot_rows(ids & 255, 256))
    results = []
    each = 16 * len(tiles)
    for place in range(len(values)):
        blocks = []
        for group in range(groups):
            start = group * each + place * 32
            blocks.append(sums[start:start + 16] + sums[start + 16:start + 32])
        results.append(jnp.concatenate(blocks, axis=1)[0:9])
    return results


def send_wanted(out_ref, precond, ids, scalar):
    cameras = precond.shape[1]
    pairs = out_ref.shape[0] // 2
    for pair in range(pairs):
        own = ids[:, pair * LANES:(pair + 1) * LANES]
        low = jnp.broadcast_to(own & (LANES - 1), (8, LANES))
        high = jnp.broadcast_to(own >> 7, (8, LANES))
        head = jnp.zeros((8, LANES), F32)
        tail = jnp.zeros((8, LANES), F32)
        for block in range(cameras // LANES):
            lanes = slice(block * LANES, (block + 1) * LANES)
            hit = high == block
            head = jnp.where(hit, take_lanes(precond[0:8, lanes], low), head)
            last = jnp.broadcast_to(precond[8:9, lanes], (8, LANES))
            tail = jnp.where(hit, take_lanes(last, low), tail)
        even, odd = pack_pair(head, tail)
        out_ref[2 * pair] = jnp.where(scalar_spot(), scalar, even)
        out_ref[2 * pair + 1] = jnp.where(scalar_spot(), scalar, odd)


def owner_start_kernel(in_ref, damp_ref, out_ref, residual_ref, scaling_ref, precond_ref, ids_ref):
    pairs = in_ref.shape[0] // 2
    rhs, diag, ids = [], [], []
    for pair in range(pairs):
        rhs.append(jnp.concatenate(unpack_pair(in_ref[2 * pair, 0:8], in_ref[2 * pair + 1, 0:8]), axis=0))
        low, high = unpack_pair(in_ref[2 * pair, 8:16], in_ref[2 * pair + 1, 8:16])
        diag.append(jnp.concatenate([low, high], axis=0))
        ids.append(high[1:2].astype(jnp.int32))
    ids = jnp.concatenate(ids, axis=1)
    ids_ref[...] = ids
    rhs = jnp.concatenate(rhs, axis=1)
    diag = jnp.concatenate(diag, axis=1)
    residual, diag = owner_sums([rhs, diag], ids, damp_ref.shape[1])
    scaling = diag + damp_ref[...]
    precond = residual / scaling
    residual_ref[...] = residual
    scaling_ref[...] = scaling
    precond_ref[...] = precond
    send_wanted(out_ref, precond, ids, sum_all(residual * precond))


def owner_image(in_ref, ids, cameras):
    image = []
    for pair in range(in_ref.shape[0] // 2):
        image.append(jnp.concatenate(unpack_pair(in_ref[2 * pair], in_ref[2 * pair + 1]), axis=0))
    return owner_sums([jnp.concatenate(image, axis=1)], ids, cameras)[0]


def owner_middle_kernel(in_ref, ids_ref, rz_ref, damp_ref, direction_ref, residual_ref, scaling_ref,
                        out_ref, update_ref, newres_ref, precond_ref):
    ids = ids_ref[...]
    direction = direction_ref[...]
    image = owner_image(in_ref, ids, damp_ref.shape[1]) + damp_ref[...] * direction
    step = rz_ref[0:1, 0:1] / carried_scalar(in_ref)
    update_ref[...] = step * direction
    residual = residual_ref[...] - step * image
    precond = residual / scaling_ref[...]
    newres_ref[...] = residual
    precond_ref[...] = precond
    send_wanted(out_ref, precond, ids, sum_all(residual * precond))


def owner_end_kernel(in_ref, ids_ref, rz_ref, damp_ref, direction_ref, residual_ref, update_ref,
                     newupdate_ref, newres_ref):
    direction = direction_ref[...]
    image = owner_image(in_ref, ids_ref[...], damp_ref.shape[1]) + damp_ref[...] * direction
    step = rz_ref[0:1, 0:1] / carried_scalar(in_ref)
    newupdate_ref[...] = update_ref[...] + step * direction
    newres_ref[...] = residual_ref[...] - step * image


def call(kernel, outs, scratch, smem, *args):
    whole = pl.BlockSpec(memory_space=pltpu.VMEM)
    specs = [pl.BlockSpec(memory_space=pltpu.SMEM) if place < smem else whole for place in range(len(args))]
    return pl.pallas_call(
        kernel,
        out_shape=[jax.ShapeDtypeStruct(shape, dtype) for shape, dtype in outs],
        in_specs=specs,
        out_specs=[whole] * len(outs),
        scratch_shapes=[pltpu.VMEM(shape, F32) for shape in scratch],
        compiler_params=pltpu.CompilerParams(vmem_limit_bytes=VMEM_BYTES),
    )(*args)


def exchange(blocks):
    return lax.all_to_all(blocks, AXES, split_axis=0, concat_axis=0, tiled=True)


def body(jac_cam, jac_pt, obs_residual, obs_point, obs_slot, request, obs_count, cam_damp, pt_damp):
    nobs = jac_cam.shape[1]
    shards = request.shape[0]
    cameras = cam_damp.shape[1]
    slots = shards * CAP
    chunk = 512
    point = obs_point.reshape(1, nobs)
    slot = obs_slot.reshape(1, nobs)
    damp_rows = pt_damp.reshape(8, LANES)
    own = ((9, cameras), F32)
    blocks = ((shards, 8, LANES), F32)
    groups = slots // 256
    sums, camp, pta, ptb, inverse = call(
        functools.partial(start_kernel, chunk),
        [((shards, 16, LANES), F32), ((32, nobs), F32), ((8, nobs), F32), ((8, nobs), F32), ((6, 8, LANES), F32)],
        [(8 * 48, LANES), (groups * 64, 256), (3, 8, LANES)],
        1, obs_count, jac_cam, jac_pt, obs_residual, point, slot, request, damp_rows)
    arrived = exchange(sums)
    send, residual, scaling, precond, ids = call(
        owner_start_kernel, [blocks, own, own, own, ((1, slots), jnp.int32)], [], 0, arrived, cam_damp)
    arrived = exchange(send)
    scratch = [(8 * 16, LANES), (groups * 32, 256), (3, 8, LANES), (8, nobs), (shards // 2, LANES)]
    scalar = ((8, LANES), F32)
    table = ((shards // 2, 16, LANES), F32)
    send, table_now, rz = call(
        functools.partial(apply_kernel, chunk, True), [blocks, table, scalar], scratch,
        1, obs_count, arrived, camp, pta, ptb, point, slot, inverse, cam_damp, precond)
    arrived = exchange(send)
    direction = precond
    send, update, residual, precond = call(
        owner_middle_kernel, [blocks, own, own, own], [], 0,
        arrived, ids, rz, cam_damp, direction, residual, scaling)
    arrived = exchange(send)
    send, direction, rz = call(
        functools.partial(apply_kernel, chunk, False), [blocks, own, scalar], scratch + [table[0]],
        1, obs_count, arrived, camp, pta, ptb, point, slot, inverse, cam_damp, precond, table_now, rz, direction)
    arrived = exchange(send)
    update, residual = call(
        owner_end_kernel, [own, own], [], 0, arrived, ids, rz, cam_damp, direction, residual, update)
    return update, residual


def solution(mesh):
    wide = P(None, AXES)
    flat = P(AXES)
    return jax.shard_map(
        body,
        mesh=mesh,
        in_specs=(wide, wide, wide, flat, flat, P(AXES, None), flat, wide, flat),
        out_specs=(wide, wide),
        check_vma=False,
    )
```

profile of v0, /device:TPU:0, one launch (start us, length us, event | category | flops | bytes accessed | tf_op | source)
XLA Modules:
  0.0 103.7 jit_solution(3647799990251666578)
XLA Ops:
  0.6 0.0 copy-start.7
  1.3 0.0 copy-done.7
  1.3 0.0 copy-start.1
  1.3 1.1 %copy-done.1 = f32[18,8192]{1,0:T(8,128)S(1)} copy-done((f32[18,8192]{1,0:T(8,128)S(1)}, f32[18,8192]{1,0:T(8,128)}, u32[]{:S(2)}) %copy-start.1) | copy-done | bytes 589848
  2.5 0.0 copy-start.2
  2.5 0.8 copy-done.2
  3.2 0.0 copy-start.3
  3.2 0.8 copy-done.3
  4.0 0.0 copy-start.4
  4.0 0.9 copy-done.4
  4.9 0.0 copy-start.5
  4.9 0.8 copy-done.5
  5.8 0.0 copy-start.6
  5.8 0.7 copy-done.6
  6.5 10.8 %shard_map.104 = (f32[32,16,128]{2,1,0:T(8,128)S(1)}, f32[32,8192]{1,0:T(8,128)S(1)}, f32[8,8192]{1,0:T(8,128)S(1)}, f32[8,8192]{1,0:T(8,128)S(1)}, f32[6,8,128]{2,1,0:T(8,128)S(1)}) custom-call(s32[1]{0:T(128)S(6)} %copy.11.count_ref.refs_0_, f32[18,8192]{1,0:T(8,128)S(1)} %copy-done.1, f32[6,8192]{1,0:T(8,128)S(1)} %copy-done.4, f32[2,8192]{1,0:T(2,128)S(1)} %copy-done.5, ...), custom_call_target="tpu_custom_call" | custom-call | tf_op jit(solution)/shard_map/pallas_call | solution.py:391
  17.3 0.0 copy-start
  17.3 17.3 %all_to_all.25.in_ref = f32[32,16,128]{2,1,0:T(8,128)S(1)} all-to-all(f32[32,16,128]{2,1,0:T(8,128)S(1)} %get-tuple-element.22), channel_id=1, replica_groups=mesh['cell'=8,'img'=4] {'cell','img'}, dimensions={0} | all-to-all | bytes 524288 | tf_op jit(solution)/shard_map/all_to_all | solution.py:402
  34.6 0.0 copy-done
  34.6 1.1 %shard_map.105 = (f32[32,8,128]{2,1,0:T(8,128)S(1)}, f32[9,768]{1,0:T(8,128)S(1)}, f32[9,768]{1,0:T(8,128)S(1)}, f32[9,768]{1,0:T(8,128)S(1)}, s32[1,2048]{1,0:T(1,128)S(1)}) custom-call(f32[32,16,128]{2,1,0:T(8,128)S(1)} %all_to_all.25.in_ref, f32[9,768]{1,0:T(8,128)S(1)} %copy-done), custom_call_target="tpu_custom_call" | custom-call | tf_op jit(solution)/shard_map/pallas_call | solution.py:391
  35.7 10.9 %all_to_all.26.refs_1_ = f32[32,8,128]{2,1,0:T(8,128)S(1)} all-to-all(f32[32,8,128]{2,1,0:T(8,128)S(1)} %get-tuple-element.23), channel_id=1, replica_groups=mesh['cell'=8,'img'=4] {'cell','img'}, dimensions={0} | all-to-all | bytes 262144 | tf_op jit(solution)/shard_map/all_to_all | solution.py:402
  46.6 12.3 %shard_map.106 = (f32[32,8,128]{2,1,0:T(8,128)S(1)}, f32[16,16,128]{2,1,0:T(8,128)S(1)}, f32[8,128]{1,0:T(8,128)S(1)}) custom-call(s32[1]{0:T(128)S(6)} %copy.11.count_ref.refs_0_, f32[32,8,128]{2,1,0:T(8,128)S(1)} %all_to_all.26.refs_1_, f32[32,8192]{1,0:T(8,128)S(1)} %get-tuple-element.24.refs_2_, f32[8,8192]{1,0:T(8,128)S(1)} %get-tuple-element.25.refs_3_, ...), custom_call_target="tpu_custom_call" | custom-call | tf_op jit(solution)/shard_map/pallas_call | solution.py:391
  58.9 10.1 %all_to_all.27.in_ref = f32[32,8,128]{2,1,0:T(8,128)S(1)} all-to-all(f32[32,8,128]{2,1,0:T(8,128)S(1)} %get-tuple-element.29), channel_id=1, replica_groups=mesh['cell'=8,'img'=4] {'cell','img'}, dimensions={0} | all-to-all | bytes 262144 | tf_op jit(solution)/shard_map/all_to_all | solution.py:402
  69.0 1.0 shard_map.107
  70.1 10.1 %all_to_all.28.refs_1_ = f32[32,8,128]{2,1,0:T(8,128)S(1)} all-to-all(f32[32,8,128]{2,1,0:T(8,128)S(1)} %get-tuple-element.34), channel_id=1, replica_groups=mesh['cell'=8,'img'=4] {'cell','img'}, dimensions={0} | all-to-all | bytes 262144 | tf_op jit(solution)/shard_map/all_to_all | solution.py:402
  80.2 12.4 %shard_map.108 = (f32[32,8,128]{2,1,0:T(8,128)S(1)}, f32[9,768]{1,0:T(8,128)S(1)}, f32[8,128]{1,0:T(8,128)S(1)}) custom-call(s32[1]{0:T(128)S(6)} %copy.11.count_ref.refs_0_, f32[32,8,128]{2,1,0:T(8,128)S(1)} %all_to_all.28.refs_1_, f32[32,8192]{1,0:T(8,128)S(1)} %get-tuple-element.24.refs_2_, f32[8,8192]{1,0:T(8,128)S(1)} %get-tuple-element.25.refs_3_, ...), custom_call_target="tpu_custom_call" | custom-call | tf_op jit(solution)/shard_map/pallas_call | solution.py:391
  92.5 10.1 %all_to_all.29.in_ref = f32[32,8,128]{2,1,0:T(8,128)S(1)} all-to-all(f32[32,8,128]{2,1,0:T(8,128)S(1)} %get-tuple-element.37), channel_id=1, replica_groups=mesh['cell'=8,'img'=4] {'cell','img'}, dimensions={0} | all-to-all | bytes 262144 | tf_op jit(solution)/shard_map/all_to_all | solution.py:402
  102.7 1.1 %shard_map.109 = (f32[9,768]{1,0:T(8,128)}, f32[9,768]{1,0:T(8,128)}) custom-call(f32[32,8,128]{2,1,0:T(8,128)S(1)} %all_to_all.29.in_ref, s32[1,2048]{1,0:T(1,128)S(1)} %get-tuple-element.30.ids_ref, f32[8,128]{1,0:T(8,128)S(1)} %get-tuple-element.38.rz_ref, f32[9,768]{1,0:T(8,128)S(1)} %copy-done, f32[9,768]{1,0:T(8,128)S(1)} %get-tuple-element.39.direction_ref, ...), custom_call_target="tpu_custom_call" | custom-call | tf_op jit(solution)/shard_map/pallas_call | solution.py:391
Async XLA Ops:
  0.6 0.7 copy-start.7
  1.3 1.1 %copy-start.1 = (f32[18,8192]{1,0:T(8,128)S(1)}, f32[18,8192]{1,0:T(8,128)}, u32[]{:S(2)}) copy-start(f32[18,8192]{1,0:T(8,128)} %cam_ref.1) | copy-start | bytes 1769476
  2.5 0.8 copy-start.2
  3.2 0.8 copy-start.3
  4.0 0.9 copy-start.4
  4.9 0.8 copy-start.5
  5.8 0.7 copy-start.6
  17.3 17.3 %copy-start = (f32[9,768]{1,0:T(8,128)S(1)}, f32[9,768]{1,0:T(8,128)}, u32[]{:S(2)}) copy-start(f32[9,768]{1,0:T(8,128)} %damp_ref.5) | copy-start | bytes 82948
where the time goes:
time: 104 us
  blocking collectives  58.6 us (56%)
  Pallas kernels  38.6 us (37%)
  local copies, waits for them, and re-layouts  5.18 us (5%)
  between operations  1.35 us (1%)
    all_to_all x5, blocking collectives, exchange(): return lax.all_to_all(blocks, AXES, split_axis=0, concat_axis=0, tiled=True)  58.6 us
    pallas_call x6, Pallas kernels, call(): pl.pallas_call(kernel, out_shape=[jax.ShapeDtypeStruct(shape, dtype) for...  38.6 us
    unnamed x16, local copies, waits for them, and re-layouts  5.18 us

commit v1 on v0

v1 whole, which is shorter than its diff:
```python
import functools

import jax
import jax.numpy as jnp
from jax import lax
from jax.experimental import pallas as pl
from jax.experimental.pallas import tpu as pltpu
from jax.sharding import PartitionSpec as P

AXES = ("cell", "img")
F32 = jnp.float32
BF16 = jnp.bfloat16
LANES = 128
CAP = 64
VMEM_BYTES = 48 * 1024 * 1024


def iota(shape, dim):
    return lax.broadcasted_iota(jnp.int32, shape, dim)


def take_lanes(table, lanes):
    return jnp.take_along_axis(table, lanes, axis=1, mode="promise_in_bounds")


def contract(left, right):
    return lax.dot_general(left, right, (((1,), (1,)), ((), ())), preferred_element_type=F32)


def one_hot_rows(index, rows):
    hit = iota((rows, index.shape[1]), 0) == index
    return jnp.where(hit, 1.0, 0.0).astype(BF16)


def rounded_parts(value, count):
    parts = []
    for _ in range(count):
        part = value.astype(BF16)
        parts.append(part)
        value = value - part.astype(F32)
    return parts


def masked_rows(rows, hit):
    return [jnp.where(hit, jnp.broadcast_to(row, hit.shape), 0.0) for row in rows]


def stack_tiles(blocks):
    if len(blocks) % 2:
        blocks = blocks + [jnp.zeros_like(blocks[0])]
    return jnp.concatenate(blocks, axis=0).astype(BF16)


def group_hits(group):
    return jnp.broadcast_to(group, (8, group.shape[1])) == iota((8, group.shape[1]), 0)


def spread_slots(heads, tails, group, groups):
    width = group.shape[1]
    tiles = [jnp.concatenate(parts, axis=0).astype(BF16) for parts in heads]
    rows = []
    wide = jnp.broadcast_to(group, (8, width))
    for number in range(groups):
        hit = jnp.where(wide == number, 1.0, 0.0)
        hit = jnp.concatenate([hit, hit], axis=0).astype(BF16)
        rows += [tile * hit for tile in tiles]
    last = []
    for base in range(0, groups, 8):
        hit = wide == iota((8, width), 0) + base
        last += masked_rows(tails, hit)
    return jnp.concatenate(rows + [stack_tiles(last)], axis=0)


def wide_parts(value, count):
    return [part.astype(F32) for part in rounded_parts(value, count)]


def swap_halves(value):
    return pltpu.roll(value, CAP, 1)


def left_half(rows=8):
    return iota((rows, LANES), 1) < CAP


def sum_all(value):
    return jnp.sum(jnp.sum(value, axis=1, keepdims=True), axis=0, keepdims=True)


def carried_scalar(ref):
    total = ref[4:5, :]
    for sender in range(1, ref.shape[0] // 5):
        total = total + ref[5 * sender + 4:5 * sender + 5, :]
    return total[:, CAP:CAP + 1]


def store_five(out_ref, pair, head, tail, scalar):
    left = left_half()
    turned = swap_halves(head)
    even = jnp.where(left, head, pltpu.roll(turned, 4, 0))
    odd = jnp.where(left, turned, pltpu.roll(head, 4, 0))
    last = jnp.broadcast_to(tail, (8, LANES))
    last_even = jnp.where(left, last, scalar)
    last_odd = jnp.where(left, swap_halves(last), scalar)
    out_ref[10 * pair:10 * pair + 4] = even[0:4]
    out_ref[10 * pair + 4:10 * pair + 5] = last_even[0:1]
    out_ref[10 * pair + 5:10 * pair + 9] = odd[0:4]
    out_ref[10 * pair + 9:10 * pair + 10] = last_odd[0:1]


def load_five(in_ref, pair):
    left = left_half(4)
    even = in_ref[10 * pair:10 * pair + 4]
    odd = in_ref[10 * pair + 5:10 * pair + 9]
    low = jnp.where(left, even, swap_halves(odd))
    high = jnp.where(left, swap_halves(even), odd)
    last_even = in_ref[10 * pair + 4:10 * pair + 5]
    last_odd = in_ref[10 * pair + 9:10 * pair + 10]
    tail = jnp.where(left_half(1), last_even, swap_halves(last_odd))
    return jnp.concatenate([low, high], axis=0), tail


def point_spread(solved_ref, low, group, jac_a, jac_b):
    low = jnp.broadcast_to(low, (8, LANES))
    hit = group_hits(group)
    first = jnp.zeros((8, LANES), F32)
    second = jnp.zeros((8, LANES), F32)
    for axis in range(3):
        taken = jnp.where(hit, take_lanes(solved_ref[axis], low), 0.0)
        first = first + jac_a[axis:axis + 1] * taken
        second = second + jac_b[axis:axis + 1] * taken
    return jnp.sum(first, axis=0, keepdims=True), jnp.sum(second, axis=0, keepdims=True)


def solve_points(inverse_ref, totals, solved_ref):
    rows = ((0, 3, 5), (3, 1, 4), (5, 4, 2))
    for axis in range(3):
        solved_ref[axis] = (
            inverse_ref[rows[axis][0]] * totals[0]
            + inverse_ref[rows[axis][1]] * totals[1]
            + inverse_ref[rows[axis][2]] * totals[2]
        )


def summed_parts(sums_ref, start, rows, count, step):
    total = sums_ref[start:start + rows, :]
    for part in range(1, count):
        begin = start + part * step
        total = total + sums_ref[begin:begin + rows, :]
    return total


def start_kernel(chunk, count_ref, cam_hbm, pt_hbm, err_hbm, point_hbm, slot_hbm, req_hbm, damp_hbm,
                 out_ref, camp_ref, pta_ref, ptb_ref, index_ref, inverse_ref,
                 psum_ref, ssum_ref, solved_ref, cam_ref, pt_ref, err_ref, point_ref, slot_ref, req_ref, damp_ref,
                 cam_sem, pt_sem, err_sem, point_sem, slot_sem, req_sem, damp_sem):
    nobs = cam_ref.shape[1]
    copies = [
        pltpu.make_async_copy(pt_hbm, pt_ref, pt_sem),
        pltpu.make_async_copy(err_hbm, err_ref, err_sem),
        pltpu.make_async_copy(point_hbm, point_ref, point_sem),
        pltpu.make_async_copy(slot_hbm, slot_ref, slot_sem),
        pltpu.make_async_copy(damp_hbm, damp_ref, damp_sem),
        pltpu.make_async_copy(cam_hbm, cam_ref, cam_sem),
        pltpu.make_async_copy(req_hbm, req_ref, req_sem),
    ]
    for copy in copies:
        copy.start()
    count = count_ref[0]
    psum_ref[...] = jnp.zeros_like(psum_ref)
    ssum_ref[...] = jnp.zeros_like(ssum_ref)
    groups = req_ref.shape[0] * CAP // 256
    for copy in copies[:5]:
        copy.wait()

    def gather_points(step, carry):
        start = pl.multiple_of(step * chunk, chunk)
        lanes = pl.ds(start, chunk)
        live = iota((1, chunk), 1) + start < count
        point = point_ref[:, lanes]
        low = point & (LANES - 1)
        group = jnp.where(live, point >> 7, -1)
        slot = slot_ref[:, lanes]
        index_ref[0:1, lanes] = low
        index_ref[1:2, lanes] = group
        index_ref[2:3, lanes] = slot
        index_ref[3:4, lanes] = jnp.where(live, slot >> 8, -1)
        jac = pt_ref[:, lanes]
        zero = jnp.zeros((1, chunk), F32)
        jac_a = jnp.concatenate([jac[0:3], zero, jac[0:3], zero], axis=0)
        jac_b = jnp.concatenate([jac[3:6], zero, jac[3:6], zero], axis=0)
        pta_ref[:, lanes] = jac_a
        ptb_ref[:, lanes] = jac_b
        turn_a = jnp.concatenate([jac[0:3], zero, jac[1:3], jac[0:1], zero], axis=0)
        turn_b = jnp.concatenate([jac[3:6], zero, jac[4:6], jac[3:4], zero], axis=0)
        err = err_ref[:, lanes]
        blocks = wide_parts(jac_a * turn_a + jac_b * turn_b, 3)
        sides = wide_parts(jac_a * err[0:1] + jac_b * err[1:2], 3)
        rows = [block[place:place + 1] for block in blocks for place in (0, 1, 2, 4, 5, 6)]
        rows += [side[place:place + 1] for side in sides for place in (0, 1, 2)]
        spread = stack_tiles(masked_rows(rows, group_hits(group)))
        psum_ref[...] += contract(spread, one_hot_rows(low, LANES))
        return carry

    lax.fori_loop(0, nobs // chunk, gather_points, 0)

    damp = damp_ref[...]
    m00, m11, m22, m01, m12, m20 = [summed_parts(psum_ref, 8 * place, 8, 3, 48) for place in range(6)]
    m00, m11, m22 = m00 + damp, m11 + damp, m22 + damp
    c00 = m11 * m22 - m12 * m12
    c01 = m12 * m20 - m01 * m22
    c02 = m01 * m12 - m11 * m20
    c11 = m22 * m00 - m20 * m20
    c12 = m20 * m01 - m12 * m00
    c22 = m00 * m11 - m01 * m01
    det = m00 * c00 + m01 * c01 + m20 * c02
    for place, cofactor in enumerate((c00, c11, c22, c01, c12, c02)):
        inverse_ref[place] = cofactor / det
    solve_points(inverse_ref, [summed_parts(psum_ref, 144 + 8 * place, 8, 3, 24) for place in range(3)], solved_ref)
    for copy in copies[5:]:
        copy.wait()

    def scatter_terms(step, carry):
        start = pl.multiple_of(step * chunk, chunk)
        lanes = pl.ds(start, chunk)
        camp_ref[0:9, lanes] = cam_ref[0:9, lanes]
        camp_ref[9:16, lanes] = jnp.zeros((7, chunk), F32)
        camp_ref[16:25, lanes] = cam_ref[9:18, lanes]
        camp_ref[25:32, lanes] = jnp.zeros((7, chunk), F32)
        kept_a, kept_b = [], []
        for tile in range(chunk // LANES):
            spot = pl.ds(start + tile * LANES, LANES)
            first, second = point_spread(
                solved_ref, index_ref[0:1, spot], index_ref[1:2, spot], pta_ref[:, spot], ptb_ref[:, spot])
            err = err_ref[:, spot]
            kept_a.append(err[0:1] - first)
            kept_b.append(err[1:2] - second)
        kept_a = jnp.concatenate(kept_a, axis=1)
        kept_b = jnp.concatenate(kept_b, axis=1)
        cam_a = camp_ref[0:16, lanes]
        cam_b = camp_ref[16:32, lanes]
        rhs = wide_parts(-(cam_a * kept_a + cam_b * kept_b), 2)
        diag = wide_parts(cam_a * cam_a + cam_b * cam_b, 2)
        heads = [[part[0:8] for part in rhs], [part[0:8] for part in diag]]
        tails = [part[8:9] for part in rhs + diag]
        slot = index_ref[2:3, lanes]
        spread = spread_slots(heads, tails, index_ref[3:4, lanes], groups)
        ssum_ref[...] += contract(spread, one_hot_rows(slot & 255, 256))
        return carry

    lax.fori_loop(0, nobs // chunk, scatter_terms, 0)
    wanted = req_ref[...].astype(F32)
    wanted = jnp.concatenate([wanted, jnp.zeros_like(wanted)], axis=1)
    left = left_half()
    for group in range(groups):
        rhs = summed_parts(ssum_ref, 32 * group, 8, 2, 8)
        diag = summed_parts(ssum_ref, 32 * group + 16, 8, 2, 8)
        last = 32 * groups + 32 * (group // 8) + group % 8
        rhs_last = summed_parts(ssum_ref, last, 1, 2, 8)
        diag_last = summed_parts(ssum_ref, last + 16, 1, 2, 8)
        for half in range(2):
            lanes = slice(half * LANES, (half + 1) * LANES)
            row = 20 * (2 * group + half)
            out_ref[row:row + 8] = jnp.where(left, rhs[:, lanes], swap_halves(diag[:, lanes]))
            out_ref[row + 10:row + 18] = jnp.where(left, swap_halves(rhs[:, lanes]), diag[:, lanes])
            left_one = left_half(1)
            out_ref[row + 8:row + 9] = jnp.where(left_one, rhs_last[:, lanes], swap_halves(diag_last[:, lanes]))
            out_ref[row + 18:row + 19] = jnp.where(left_one, swap_halves(rhs_last[:, lanes]), diag_last[:, lanes])
            owner = 4 * group + 2 * half
            out_ref[row + 9:row + 10] = wanted[owner:owner + 1]
            out_ref[row + 19:row + 20] = wanted[owner + 1:owner + 2]


def apply_kernel(chunk, first, *refs):
    if first:
        (in_ref, camp_ref, pta_ref, ptb_ref, index_ref, inverse_ref, damp_ref, precond_ref,
         out_ref, table_ref, last_ref, rz_ref, psum_ref, ssum_ref, solved_ref, along_ref) = refs
    else:
        (in_ref, camp_ref, pta_ref, ptb_ref, index_ref, inverse_ref, damp_ref, precond_ref,
         oldtable_ref, oldlast_ref, oldrz_ref, oldown_ref,
         out_ref, own_ref, rz_ref, psum_ref, ssum_ref, solved_ref, along_ref, table_ref, last_ref) = refs
    nobs = camp_ref.shape[1]
    psum_ref[...] = jnp.zeros_like(psum_ref)
    ssum_ref[...] = jnp.zeros_like(ssum_ref)
    pairs = table_ref.shape[0]
    groups = pairs // 2
    rz = carried_scalar(in_ref)
    rz_ref[...] = jnp.broadcast_to(rz, rz_ref.shape)
    own = precond_ref[...]
    if not first:
        beta = rz / oldrz_ref[0:1, 0:1]
        own = own + beta * oldown_ref[...]
        own_ref[...] = own
    for pair in range(pairs):
        head, tail = load_five(in_ref, pair)
        if not first:
            head = head + beta * oldtable_ref[pair]
            tail = tail + beta * oldlast_ref[pair:pair + 1]
        table_ref[pair] = head
        last_ref[pair:pair + 1] = tail

    def gather_points(step, carry):
        start = pl.multiple_of(step * chunk, chunk)
        lanes = pl.ds(start, chunk)
        for tile in range(chunk // LANES):
            spot = pl.ds(start + tile * LANES, LANES)
            slot = index_ref[2:3, spot]
            low = jnp.broadcast_to(slot & (LANES - 1), (8, LANES))
            high = jnp.broadcast_to(slot >> 7, (8, LANES))
            taken = jnp.zeros((8, LANES), F32)
            for pair in range(pairs):
                taken = jnp.where(high == pair, take_lanes(table_ref[pair], low), taken)
            tail = jnp.zeros((8, LANES), F32)
            for base in range(0, pairs, 8):
                hit = high == iota((8, LANES), 0) + base
                tail = jnp.where(hit, take_lanes(last_ref[base:base + 8], low), tail)
            tail = jnp.sum(tail, axis=0, keepdims=True)
            along_ref[0:1, spot] = jnp.sum(camp_ref[0:8, spot] * taken, axis=0, keepdims=True) + camp_ref[8:9, spot] * tail
            along_ref[1:2, spot] = jnp.sum(camp_ref[16:24, spot] * taken, axis=0, keepdims=True) + camp_ref[24:25, spot] * tail
        sides = wide_parts(pta_ref[:, lanes] * along_ref[0:1, lanes] + ptb_ref[:, lanes] * along_ref[1:2, lanes], 3)
        rows = [side[place:place + 1] for side in sides for place in (0, 1, 2)]
        spread = stack_tiles(masked_rows(rows, group_hits(index_ref[1:2, lanes])))
        psum_ref[...] += contract(spread, one_hot_rows(index_ref[0:1, lanes], LANES))
        return carry

    lax.fori_loop(0, nobs // chunk, gather_points, 0)
    solve_points(inverse_ref, [summed_parts(psum_ref, 8 * place, 8, 3, 24) for place in range(3)], solved_ref)

    def scatter_terms(step, carry):
        start = pl.multiple_of(step * chunk, chunk)
        lanes = pl.ds(start, chunk)
        kept_a, kept_b = [], []
        for tile in range(chunk // LANES):
            spot = pl.ds(start + tile * LANES, LANES)
            first_sum, second_sum = point_spread(
                solved_ref, index_ref[0:1, spot], index_ref[1:2, spot], pta_ref[:, spot], ptb_ref[:, spot])
            kept_a.append(along_ref[0:1, spot] - first_sum)
            kept_b.append(along_ref[1:2, spot] - second_sum)
        kept_a = jnp.concatenate(kept_a, axis=1)
        kept_b = jnp.concatenate(kept_b, axis=1)
        terms = wide_parts(camp_ref[0:16, lanes] * kept_a + camp_ref[16:32, lanes] * kept_b, 2)
        group = index_ref[3:4, lanes]
        spread = spread_slots([[part[0:8] for part in terms]], [part[8:9] for part in terms], group, groups)
        ssum_ref[...] += contract(spread, one_hot_rows(index_ref[2:3, lanes] & 255, 256))
        energy = along_ref[0:1, lanes] * kept_a + along_ref[1:2, lanes] * kept_b
        return carry + jnp.where(group >= 0, energy, 0.0)

    energy = lax.fori_loop(0, nobs // chunk, scatter_terms, jnp.zeros((1, chunk), F32))
    partial = sum_all(energy) + sum_all(damp_ref[...] * own * own)
    for group in range(groups):
        head = summed_parts(ssum_ref, 16 * group, 8, 2, 8)
        tail = summed_parts(ssum_ref, 16 * groups + 16 * (group // 8) + group % 8, 1, 2, 8)
        for half in range(2):
            lanes = slice(half * LANES, (half + 1) * LANES)
            store_five(out_ref, 2 * group + half, head[:, lanes], tail[:, lanes], partial)


def owner_sums(values, ids, cameras):
    groups = cameras // 256
    tiles = []
    for value in values:
        parts = wide_parts(value, 2)
        tiles.append(jnp.concatenate(parts, axis=0).astype(BF16))
    rows = []
    for number in range(groups):
        hit = jnp.where(jnp.broadcast_to(ids >> 8, tiles[0].shape) == number, 1.0, 0.0).astype(BF16)
        rows += [tile * hit for tile in tiles]
    sums = contract(jnp.concatenate(rows, axis=0), one_hot_rows(ids & 255, 256))
    results = []
    height = values[0].shape[0]
    each = 2 * height * len(tiles)
    for place in range(len(values)):
        blocks = []
        for group in range(groups):
            start = group * each + place * 2 * height
            blocks.append(sums[start:start + height] + sums[start + height:start + 2 * height])
        results.append(jnp.concatenate(blocks, axis=1)[0:9])
    return results


def send_wanted(out_ref, precond, ids, scalar):
    cameras = precond.shape[1]
    for pair in range(out_ref.shape[0] // 10):
        own = ids[:, pair * LANES:(pair + 1) * LANES]
        low = jnp.broadcast_to(own & (LANES - 1), (8, LANES))
        high = jnp.broadcast_to(own >> 7, (8, LANES))
        head = jnp.zeros((8, LANES), F32)
        tail = jnp.zeros((8, LANES), F32)
        for block in range(cameras // LANES):
            lanes = slice(block * LANES, (block + 1) * LANES)
            hit = high == block
            head = jnp.where(hit, take_lanes(precond[0:8, lanes], low), head)
            last = jnp.broadcast_to(precond[8:9, lanes], (8, LANES))
            tail = jnp.where(hit, take_lanes(last, low), tail)
        store_five(out_ref, pair, head, tail[0:1], scalar)


def owner_start_kernel(in_ref, damp_ref, out_ref, residual_ref, scaling_ref, precond_ref, ids_ref):
    rhs, diag, ids = [], [], []
    left = left_half(9)
    for pair in range(in_ref.shape[0] // 20):
        even = in_ref[20 * pair:20 * pair + 9]
        odd = in_ref[20 * pair + 10:20 * pair + 19]
        low = jnp.where(left, even, swap_halves(odd))
        high = jnp.where(left, swap_halves(even), odd)
        pad = jnp.zeros((7, LANES), F32)
        rhs.append(jnp.concatenate([low, pad], axis=0))
        diag.append(jnp.concatenate([high, pad], axis=0))
        even = in_ref[20 * pair + 9:20 * pair + 10]
        odd = in_ref[20 * pair + 19:20 * pair + 20]
        ids.append(jnp.where(left_half(1), even, swap_halves(odd)).astype(jnp.int32))
    ids = jnp.concatenate(ids, axis=1)
    ids_ref[...] = ids
    rhs = jnp.concatenate(rhs, axis=1)
    diag = jnp.concatenate(diag, axis=1)
    residual, diag = owner_sums([rhs, diag], ids, damp_ref.shape[1])
    scaling = diag + damp_ref[...]
    precond = residual / scaling
    residual_ref[...] = residual
    scaling_ref[...] = scaling
    precond_ref[...] = precond
    send_wanted(out_ref, precond, ids, sum_all(residual * precond))


def owner_image(in_ref, ids, cameras):
    image = []
    pad = jnp.zeros((7, LANES), F32)
    for pair in range(in_ref.shape[0] // 10):
        head, tail = load_five(in_ref, pair)
        image.append(jnp.concatenate([head, tail, pad], axis=0))
    return owner_sums([jnp.concatenate(image, axis=1)], ids, cameras)[0]


def owner_middle_kernel(in_ref, ids_ref, rz_ref, damp_ref, direction_ref, residual_ref, scaling_ref,
                        out_ref, update_ref, newres_ref, precond_ref):
    ids = ids_ref[...]
    direction = direction_ref[...]
    image = owner_image(in_ref, ids, damp_ref.shape[1]) + damp_ref[...] * direction
    step = rz_ref[0:1, 0:1] / carried_scalar(in_ref)
    update_ref[...] = step * direction
    residual = residual_ref[...] - step * image
    precond = residual / scaling_ref[...]
    newres_ref[...] = residual
    precond_ref[...] = precond
    send_wanted(out_ref, precond, ids, sum_all(residual * precond))


def owner_end_kernel(in_ref, ids_ref, rz_ref, damp_ref, direction_ref, residual_ref, update_ref,
                     newupdate_ref, newres_ref):
    direction = direction_ref[...]
    image = owner_image(in_ref, ids_ref[...], damp_ref.shape[1]) + damp_ref[...] * direction
    step = rz_ref[0:1, 0:1] / carried_scalar(in_ref)
    newupdate_ref[...] = update_ref[...] + step * direction
    newres_ref[...] = residual_ref[...] - step * image


def call(kernel, outs, scratch, *args, smem=0, hbm=0):
    whole = pl.BlockSpec(memory_space=pltpu.VMEM)
    specs = [pl.BlockSpec(memory_space=pltpu.SMEM)] * smem + [pl.BlockSpec(memory_space=pltpu.HBM)] * hbm
    specs += [whole] * (len(args) - smem - hbm)
    return pl.pallas_call(
        kernel,
        out_shape=[jax.ShapeDtypeStruct(shape, dtype) for shape, dtype in outs],
        in_specs=specs,
        out_specs=[whole] * len(outs),
        scratch_shapes=scratch,
        compiler_params=pltpu.CompilerParams(vmem_limit_bytes=VMEM_BYTES),
    )(*args)


def exchange(blocks, shards):
    moved = lax.all_to_all(blocks.reshape(shards, 1, -1), AXES, split_axis=0, concat_axis=0, tiled=True)
    return moved.reshape(blocks.shape)


def start_call(chunk, *args):
    _, jac_cam, _, _, _, _, request, _ = args
    nobs = jac_cam.shape[1]
    shards = request.shape[0]
    groups = shards * CAP // 256
    copied = args[1:]
    scratch = [pltpu.VMEM((224, LANES), F32), pltpu.VMEM((groups * 32 + (groups + 7) // 8 * 32, 256), F32),
               pltpu.VMEM((3, 8, LANES), F32)]
    scratch += [pltpu.VMEM(arg.shape, arg.dtype) for arg in copied]
    scratch += [pltpu.SemaphoreType.DMA] * len(copied)
    outs = [((shards * 10, LANES), F32), ((32, nobs), F32), ((8, nobs), F32), ((8, nobs), F32),
            ((8, nobs), jnp.int32), ((6, 8, LANES), F32)]
    return call(functools.partial(start_kernel, chunk), outs, scratch, *args, smem=1, hbm=len(copied))


def apply_call(chunk, first, *args):
    arrived, camp = args[:2]
    nobs = camp.shape[1]
    shards = arrived.shape[0] // 5
    pairs = shards // 2
    groups = shards // 4
    cameras = args[6].shape[1]
    scratch = [pltpu.VMEM((80, LANES), F32), pltpu.VMEM((groups * 16 + (groups + 7) // 8 * 16, 256), F32),
               pltpu.VMEM((3, 8, LANES), F32), pltpu.VMEM((8, nobs), F32)]
    table = (pairs, 8, LANES)
    last = ((pairs + 7) // 8 * 8, LANES)
    scalar = ((8, LANES), F32)
    sent = ((shards * 5, LANES), F32)
    if first:
        outs = [sent, (table, F32), (last, F32), scalar]
    else:
        outs = [sent, ((9, cameras), F32), scalar]
        scratch += [pltpu.VMEM(table, F32), pltpu.VMEM(last, F32)]
    return call(functools.partial(apply_kernel, chunk, first), outs, scratch, *args)


def body(jac_cam, jac_pt, obs_residual, obs_point, obs_slot, request, obs_count, cam_damp, pt_damp):
    nobs = jac_cam.shape[1]
    shards = request.shape[0]
    cameras = cam_damp.shape[1]
    slots = shards * CAP
    chunk = 4096
    own = ((9, cameras), F32)
    sent = ((shards * 5, LANES), F32)
    sums, camp, pta, ptb, index, inverse = start_call(
        chunk, obs_count, jac_cam, jac_pt, obs_residual, obs_point.reshape(1, nobs), obs_slot.reshape(1, nobs),
        request, pt_damp.reshape(8, LANES))
    arrived = exchange(sums, shards)
    send, residual, scaling, precond, ids = call(
        owner_start_kernel, [sent, own, own, own, ((1, slots), jnp.int32)], [], arrived, cam_damp)
    arrived = exchange(send, shards)
    send, table, last, rz = apply_call(
        chunk, True, arrived, camp, pta, ptb, index, inverse, cam_damp, precond)
    arrived = exchange(send, shards)
    direction = precond
    send, update, residual, precond = call(
        owner_middle_kernel, [sent, own, own, own], [],
        arrived, ids, rz, cam_damp, direction, residual, scaling)
    arrived = exchange(send, shards)
    send, direction, rz = apply_call(
        chunk, False, arrived, camp, pta, ptb, index, inverse, cam_damp, precond, table, last, rz, direction)
    arrived = exchange(send, shards)
    update, residual = call(
        owner_end_kernel, [own, own], [], arrived, ids, rz, cam_damp, direction, residual, update)
    return update, residual


def solution(mesh):
    wide = P(None, AXES)
    flat = P(AXES)
    return jax.shard_map(
        body,
        mesh=mesh,
        in_specs=(wide, wide, wide, flat, flat, P(AXES, None), flat, wide, flat),
        out_specs=(wide, wide),
        check_vma=False,
    )
```

time: 104 us -> 79.2 us (0.76)
  Pallas kernels: 38.6 us -> 18.4 us
  blocking collectives: 58.6 us -> 53.7 us
    pallas_call x6, Pallas kernels: 38.6 us -> 18.4 us  [call(): pl.pallas_call(kernel, out_shape=[jax.ShapeDtypeStruct(shape, dtype) for...]
    all_to_all x5, blocking collectives: 58.6 us -> 53.7 us  [exchange(): lax.all_to_all(blocks.reshape(shards, 1, -1), AXES, split_axis=0, concat_...]
where the time goes in v1:
time: 79.2 us; the launch traced here: 78.6 us
  blocking collectives  53.7 us (68%)
  Pallas kernels  18.4 us (23%)
  local copies, waits for them, and re-layouts  5.18 us (7%)
  between operations  1.34 us (2%)
    all_to_all x5, blocking collectives, exchange(): lax.all_to_all(blocks.reshape(shards, 1, -1), AXES, split_axis=0, concat_...  53.7 us
    pallas_call x6, Pallas kernels, call(): pl.pallas_call(kernel, out_shape=[jax.ShapeDtypeStruct(shape, dtype) for...  18.4 us
    unnamed x16, local copies, waits for them, and re-layouts  5.18 us

profile of v1, /device:TPU:0, one launch (start us, length us, event | category | flops | bytes accessed | tf_op | source)
XLA Modules:
  0.0 78.6 jit_solution(6436905930156065260)
XLA Ops:
  0.6 0.0 copy-start.7
  1.3 0.0 copy-done.7
  1.3 0.0 copy-start.1
  1.3 1.1 %copy-done.1 = f32[18,8192]{1,0:T(8,128)S(1)} copy-done((f32[18,8192]{1,0:T(8,128)S(1)}, f32[18,8192]{1,0:T(8,128)}, u32[]{:S(2)}) %copy-start.1) | copy-done | bytes 589848
  2.5 0.0 copy-start.2
  2.5 0.9 %copy-done.2 = f32[6,8192]{1,0:T(8,128)S(1)} copy-done((f32[6,8192]{1,0:T(8,128)S(1)}, f32[6,8192]{1,0:T(8,128)}, u32[]{:S(2)}) %copy-start.2) | copy-done | bytes 196632
  3.4 0.0 copy-start.3
  3.4 0.8 %copy-done.3 = f32[2,8192]{1,0:T(2,128)S(1)} copy-done((f32[2,8192]{1,0:T(2,128)S(1)}, f32[2,8192]{1,0:T(2,128)}, u32[]{:S(2)}) %copy-start.3) | copy-done | bytes 65560
  4.2 0.0 copy-start.4
  4.2 0.8 copy-done.4
  5.0 0.0 copy-start.5
  5.0 0.8 copy-done.5
  5.8 0.0 copy-start.6
  5.8 0.7 copy-done.6
  6.5 4.2 %shard_map.104 = (f32[320,128]{1,0:T(8,128)S(1)}, f32[32,8192]{1,0:T(8,128)S(1)}, f32[8,8192]{1,0:T(8,128)S(1)}, f32[8,8192]{1,0:T(8,128)S(1)}, s32[8,8192]{1,0:T(8,128)S(1)}, /*index=5*/f32[6,8,128]{2,1,0:T(8,128)S(1)}) custom-call(s32[1]{0:T(128)S(6)} %copy.16.count_ref, f32[18,8192]{1,0:T(8,128)S(1)} %copy-done.1, f32[6,8192]{1,0:T(8,128)S(1)} %copy-done.2, ...), custom_call_target="tpu_custom_call" | custom-call | tf_op jit(solution)/shard_map/pallas_call | solution.py:461
  10.7 0.0 copy-start
  10.7 16.0 %all_to_all.25 = f32[32,1,1280]{2,1,0:T(1,128)S(1)} all-to-all(f32[32,1,1280]{2,1,0:T(1,128)S(1)} %bitcast.18), channel_id=1, replica_groups=mesh['cell'=8,'img'=4] {'cell','img'}, dimensions={0} | all-to-all | bytes 327680 | tf_op jit(solution)/shard_map/all_to_all | solution.py:472
  26.7 0.0 copy-done
  26.7 1.1 %shard_map.105 = (f32[160,128]{1,0:T(8,128)S(1)}, f32[9,768]{1,0:T(8,128)S(1)}, f32[9,768]{1,0:T(8,128)S(1)}, f32[9,768]{1,0:T(8,128)S(1)}, s32[1,2048]{1,0:T(1,128)S(1)}) custom-call(f32[320,128]{1,0:T(8,128)S(1)} %bitcast.13, f32[9,768]{1,0:T(8,128)S(1)} %copy-done), custom_call_target="tpu_custom_call" | custom-call | tf_op jit(solution)/shard_map/pallas_call | solution.py:461
  27.8 9.5 %all_to_all.26 = f32[32,1,640]{2,1,0:T(1,128)S(1)} all-to-all(f32[32,1,640]{2,1,0:T(1,128)S(1)} %bitcast.21), channel_id=1, replica_groups=mesh['cell'=8,'img'=4] {'cell','img'}, dimensions={0} | all-to-all | bytes 163840 | tf_op jit(solution)/shard_map/all_to_all | solution.py:472
  37.3 5.5 %shard_map.106 = (f32[160,128]{1,0:T(8,128)S(1)}, f32[16,8,128]{2,1,0:T(8,128)S(1)}, f32[16,128]{1,0:T(8,128)S(1)}, f32[8,128]{1,0:T(8,128)S(1)}) custom-call(f32[160,128]{1,0:T(8,128)S(1)} %bitcast.15, f32[32,8192]{1,0:T(8,128)S(1)} %get-tuple-element.26.refs_1_, f32[8,8192]{1,0:T(8,128)S(1)} %get-tuple-element.27.refs_2_, ...), custom_call_target="tpu_custom_call" | custom-call | tf_op jit(solution)/shard_map/pallas_call | solution.py:461
  42.8 9.4 %all_to_all.27 = f32[32,1,640]{2,1,0:T(1,128)S(1)} all-to-all(f32[32,1,640]{2,1,0:T(1,128)S(1)} %bitcast.22), channel_id=1, replica_groups=mesh['cell'=8,'img'=4] {'cell','img'}, dimensions={0} | all-to-all | bytes 163840 | tf_op jit(solution)/shard_map/all_to_all | solution.py:472
  52.2 1.0 %shard_map.107 = (f32[160,128]{1,0:T(8,128)S(1)}, f32[9,768]{1,0:T(8,128)S(1)}, f32[9,768]{1,0:T(8,128)S(1)}, f32[9,768]{1,0:T(8,128)S(1)}) custom-call(f32[160,128]{1,0:T(8,128)S(1)} %bitcast.17, s32[1,2048]{1,0:T(1,128)S(1)} %get-tuple-element.33.ids_ref, f32[8,128]{1,0:T(8,128)S(1)} %get-tuple-element.34.rz_ref.refs_10_, f32[9,768]{1,0:T(8,128)S(1)} %copy-done, ...), custom_call_target="tpu_custom_call" | custom-call | tf_op jit(solution)/shard_map/pallas_call | solution.py:461
  53.2 9.4 %all_to_all.28 = f32[32,1,640]{2,1,0:T(1,128)S(1)} all-to-all(f32[32,1,640]{2,1,0:T(1,128)S(1)} %bitcast.20), channel_id=1, replica_groups=mesh['cell'=8,'img'=4] {'cell','img'}, dimensions={0} | all-to-all | bytes 163840 | tf_op jit(solution)/shard_map/all_to_all | solution.py:472
  62.6 5.5 %shard_map.108 = (f32[160,128]{1,0:T(8,128)S(1)}, f32[9,768]{1,0:T(8,128)S(1)}, f32[8,128]{1,0:T(8,128)S(1)}) custom-call(f32[160,128]{1,0:T(8,128)S(1)} %bitcast.14, f32[32,8192]{1,0:T(8,128)S(1)} %get-tuple-element.26.refs_1_, f32[8,8192]{1,0:T(8,128)S(1)} %get-tuple-element.27.refs_2_, f32[8,8192]{1,0:T(8,128)S(1)} %get-tuple-element.28.refs_3_, ...), custom_call_target="tpu_custom_call" | custom-call | tf_op jit(solution)/shard_map/pallas_call | solution.py:461
  68.1 9.4 %all_to_all.29 = f32[32,1,640]{2,1,0:T(1,128)S(1)} all-to-all(f32[32,1,640]{2,1,0:T(1,128)S(1)} %bitcast.19), channel_id=1, replica_groups=mesh['cell'=8,'img'=4] {'cell','img'}, dimensions={0} | all-to-all | bytes 163840 | tf_op jit(solution)/shard_map/all_to_all | solution.py:472
  77.6 1.1 %shard_map.109 = (f32[9,768]{1,0:T(8,128)}, f32[9,768]{1,0:T(8,128)}) custom-call(f32[160,128]{1,0:T(8,128)S(1)} %bitcast.16, s32[1,2048]{1,0:T(1,128)S(1)} %get-tuple-element.33.ids_ref, f32[8,128]{1,0:T(8,128)S(1)} %get-tuple-element.42.rz_ref, f32[9,768]{1,0:T(8,128)S(1)} %copy-done, f32[9,768]{1,0:T(8,128)S(1)} %get-tuple-element.43.direction_ref, ...), custom_call_target="tpu_custom_call" | custom-call | tf_op jit(solution)/shard_map/pallas_call | solution.py:461
Async XLA Ops:
  0.6 0.7 copy-start.7
  1.3 1.1 %copy-start.1 = (f32[18,8192]{1,0:T(8,128)S(1)}, f32[18,8192]{1,0:T(8,128)}, u32[]{:S(2)}) copy-start(f32[18,8192]{1,0:T(8,128)} %cam_hbm.1) | copy-start | bytes 1769476
  2.5 0.9 %copy-start.2 = (f32[6,8192]{1,0:T(8,128)S(1)}, f32[6,8192]{1,0:T(8,128)}, u32[]{:S(2)}) copy-start(f32[6,8192]{1,0:T(8,128)} %pt_hbm.1) | copy-start | bytes 589828
  3.4 0.8 %copy-start.3 = (f32[2,8192]{1,0:T(2,128)S(1)}, f32[2,8192]{1,0:T(2,128)}, u32[]{:S(2)}) copy-start(f32[2,8192]{1,0:T(2,128)} %err_hbm.1) | copy-start | bytes 196612
  4.2 0.8 copy-start.4
  5.0 0.8 copy-start.5
  5.8 0.7 copy-start.6
  10.7 16.0 %copy-start = (f32[9,768]{1,0:T(8,128)S(1)}, f32[9,768]{1,0:T(8,128)}, u32[]{:S(2)}) copy-start(f32[9,768]{1,0:T(8,128)} %damp_ref.5) | copy-start | bytes 82948

commit v2 on v1

--- a/solution.py
+++ b/solution.py
@@ -485,7 +485,8 @@
     scratch += [pltpu.SemaphoreType.DMA] * len(copied)
     outs = [((shards * 10, LANES), F32), ((32, nobs), F32), ((8, nobs), F32), ((8, nobs), F32),
             ((8, nobs), jnp.int32), ((6, 8, LANES), F32)]
-    return call(functools.partial(start_kernel, chunk), outs, scratch, *args, smem=1, hbm=len(copied))
+    copied = [pltpu.with_memory_space_constraint(arg, pltpu.HBM) for arg in copied]
+    return call(functools.partial(start_kernel, chunk), outs, scratch, args[0], *copied, smem=1, hbm=len(copied))
 
 
 def apply_call(chunk, first, *args):

time: 79.2 us -> 74.4 us (0.939)
  local copies, waits for them, and re-layouts: 5.18 us -> 0.01 us
    unnamed x16 -> x2, local copies, waits for them, and re-layouts: 5.18 us -> 0.01 us
where the time goes in v2:
time: 74.4 us; the launch traced here: 74.1 us
  blocking collectives  53.7 us (72%)
  Pallas kernels  19.1 us (26%)
  between operations  1.32 us (2%)
    all_to_all x5, blocking collectives, exchange(): lax.all_to_all(blocks.reshape(shards, 1, -1), AXES, split_axis=0, concat_...  53.7 us
    pallas_call x6, Pallas kernels, call(): pl.pallas_call(kernel, out_shape=[jax.ShapeDtypeStruct(shape, dtype) for...  19.1 us

profile of v2, /device:TPU:0, one launch (start us, length us, event | category | flops | bytes accessed | tf_op | source)
XLA Modules:
  0.0 74.1 jit_solution(2795767517929100624)
XLA Ops:
  1.3 4.9 %shard_map.104 = (f32[320,128]{1,0:T(8,128)S(1)}, f32[32,8192]{1,0:T(8,128)S(1)}, f32[8,8192]{1,0:T(8,128)S(1)}, f32[8,8192]{1,0:T(8,128)S(1)}, s32[8,8192]{1,0:T(8,128)S(1)}, /*index=5*/f32[6,8,128]{2,1,0:T(8,128)S(1)}) custom-call(s32[1]{0:T(128)S(6)} %copy.16.count_ref, f32[18,8192]{1,0:T(8,128)} %cam_hbm.1, f32[6,8192]{1,0:T(8,128)} %pt_hbm.1, ...), custom_call_target="tpu_custom_call" | custom-call | tf_op jit(solution)/shard_map/pallas_call | solution.py:461
  6.2 0.0 copy-start
  6.2 16.0 %all_to_all.25 = f32[32,1,1280]{2,1,0:T(1,128)S(1)} all-to-all(f32[32,1,1280]{2,1,0:T(1,128)S(1)} %bitcast.18), channel_id=1, replica_groups=mesh['cell'=8,'img'=4] {'cell','img'}, dimensions={0} | all-to-all | bytes 327680 | tf_op jit(solution)/shard_map/all_to_all | solution.py:472
  22.2 0.0 copy-done
  22.2 1.1 %shard_map.105 = (f32[160,128]{1,0:T(8,128)S(1)}, f32[9,768]{1,0:T(8,128)S(1)}, f32[9,768]{1,0:T(8,128)S(1)}, f32[9,768]{1,0:T(8,128)S(1)}, s32[1,2048]{1,0:T(1,128)S(1)}) custom-call(f32[320,128]{1,0:T(8,128)S(1)} %bitcast.13, f32[9,768]{1,0:T(8,128)S(1)} %copy-done), custom_call_target="tpu_custom_call" | custom-call | tf_op jit(solution)/shard_map/pallas_call | solution.py:461
  23.3 9.5 %all_to_all.26 = f32[32,1,640]{2,1,0:T(1,128)S(1)} all-to-all(f32[32,1,640]{2,1,0:T(1,128)S(1)} %bitcast.21), channel_id=1, replica_groups=mesh['cell'=8,'img'=4] {'cell','img'}, dimensions={0} | all-to-all | bytes 163840 | tf_op jit(solution)/shard_map/all_to_all | solution.py:472
  32.8 5.5 %shard_map.106 = (f32[160,128]{1,0:T(8,128)S(1)}, f32[16,8,128]{2,1,0:T(8,128)S(1)}, f32[16,128]{1,0:T(8,128)S(1)}, f32[8,128]{1,0:T(8,128)S(1)}) custom-call(f32[160,128]{1,0:T(8,128)S(1)} %bitcast.15, f32[32,8192]{1,0:T(8,128)S(1)} %get-tuple-element.26.refs_1_, f32[8,8192]{1,0:T(8,128)S(1)} %get-tuple-element.27.refs_2_, ...), custom_call_target="tpu_custom_call" | custom-call | tf_op jit(solution)/shard_map/pallas_call | solution.py:461
  38.3 9.4 %all_to_all.27 = f32[32,1,640]{2,1,0:T(1,128)S(1)} all-to-all(f32[32,1,640]{2,1,0:T(1,128)S(1)} %bitcast.22), channel_id=1, replica_groups=mesh['cell'=8,'img'=4] {'cell','img'}, dimensions={0} | all-to-all | bytes 163840 | tf_op jit(solution)/shard_map/all_to_all | solution.py:472
  47.7 1.0 %shard_map.107 = (f32[160,128]{1,0:T(8,128)S(1)}, f32[9,768]{1,0:T(8,128)S(1)}, f32[9,768]{1,0:T(8,128)S(1)}, f32[9,768]{1,0:T(8,128)S(1)}) custom-call(f32[160,128]{1,0:T(8,128)S(1)} %bitcast.17, s32[1,2048]{1,0:T(1,128)S(1)} %get-tuple-element.33.ids_ref, f32[8,128]{1,0:T(8,128)S(1)} %get-tuple-element.34.rz_ref.refs_10_, f32[9,768]{1,0:T(8,128)S(1)} %copy-done, ...), custom_call_target="tpu_custom_call" | custom-call | tf_op jit(solution)/shard_map/pallas_call | solution.py:461
  48.7 9.4 %all_to_all.28 = f32[32,1,640]{2,1,0:T(1,128)S(1)} all-to-all(f32[32,1,640]{2,1,0:T(1,128)S(1)} %bitcast.20), channel_id=1, replica_groups=mesh['cell'=8,'img'=4] {'cell','img'}, dimensions={0} | all-to-all | bytes 163840 | tf_op jit(solution)/shard_map/all_to_all | solution.py:472
  58.1 5.5 %shard_map.108 = (f32[160,128]{1,0:T(8,128)S(1)}, f32[9,768]{1,0:T(8,128)S(1)}, f32[8,128]{1,0:T(8,128)S(1)}) custom-call(f32[160,128]{1,0:T(8,128)S(1)} %bitcast.14, f32[32,8192]{1,0:T(8,128)S(1)} %get-tuple-element.26.refs_1_, f32[8,8192]{1,0:T(8,128)S(1)} %get-tuple-element.27.refs_2_, f32[8,8192]{1,0:T(8,128)S(1)} %get-tuple-element.28.refs_3_, ...), custom_call_target="tpu_custom_call" | custom-call | tf_op jit(solution)/shard_map/pallas_call | solution.py:461
  63.6 9.4 %all_to_all.29 = f32[32,1,640]{2,1,0:T(1,128)S(1)} all-to-all(f32[32,1,640]{2,1,0:T(1,128)S(1)} %bitcast.19), channel_id=1, replica_groups=mesh['cell'=8,'img'=4] {'cell','img'}, dimensions={0} | all-to-all | bytes 163840 | tf_op jit(solution)/shard_map/all_to_all | solution.py:472
  73.0 1.1 %shard_map.109 = (f32[9,768]{1,0:T(8,128)}, f32[9,768]{1,0:T(8,128)}) custom-call(f32[160,128]{1,0:T(8,128)S(1)} %bitcast.16, s32[1,2048]{1,0:T(1,128)S(1)} %get-tuple-element.33.ids_ref, f32[8,128]{1,0:T(8,128)S(1)} %get-tuple-element.42.rz_ref, f32[9,768]{1,0:T(8,128)S(1)} %copy-done, f32[9,768]{1,0:T(8,128)S(1)} %get-tuple-element.43.direction_ref, ...), custom_call_target="tpu_custom_call" | custom-call | tf_op jit(solution)/shard_map/pallas_call | solution.py:461
Async XLA Ops:
  6.2 16.0 %copy-start = (f32[9,768]{1,0:T(8,128)S(1)}, f32[9,768]{1,0:T(8,128)}, u32[]{:S(2)}) copy-start(f32[9,768]{1,0:T(8,128)} %damp_ref.5) | copy-start | bytes 82948

commit v3 on v2

--- a/solution.py
+++ b/solution.py
@@ -12,7 +12,7 @@
 BF16 = jnp.bfloat16
 LANES = 128
 CAP = 64
-VMEM_BYTES = 48 * 1024 * 1024
+VMEM_BYTES = 32 * 1024 * 1024
 
 
 def iota(shape, dim):
@@ -30,6 +30,13 @@
 def one_hot_rows(index, rows):
     hit = iota((rows, index.shape[1]), 0) == index
     return jnp.where(hit, 1.0, 0.0).astype(BF16)
+
+
+def one_hot_columns(index, columns):
+    spread = jnp.broadcast_to(index.astype(F32), (LANES, LANES)).astype(BF16).T
+    spread = jnp.concatenate([spread] * (columns // LANES), axis=1)
+    lane = iota((LANES, columns), 1).astype(F32).astype(BF16)
+    return jnp.where(spread == lane, jnp.ones((), BF16), jnp.zeros((), BF16))
 
 
 def rounded_parts(value, count):
@@ -120,16 +127,51 @@
     return jnp.concatenate([low, high], axis=0), tail
 
 
-def point_spread(solved_ref, low, group, jac_a, jac_b):
+def pipelined(steps, build, product):
+    for step in range(steps):
+        build(step)
+        if step:
+            product(step - 1)
+    product(steps - 1)
+
+
+def chunk_lanes(step, chunk):
+    return slice(step * chunk, (step + 1) * chunk)
+
+
+def add_product(sums_ref, left_ref, right_ref, lanes, first):
+    product = jnp.dot(left_ref[:, lanes], right_ref[lanes, :], preferred_element_type=F32)
+    if first:
+        sums_ref[...] = product
+    else:
+        sums_ref[...] += product
+
+
+def point_spread(solved_ref, low, group, jac):
     low = jnp.broadcast_to(low, (8, LANES))
     hit = group_hits(group)
     first = jnp.zeros((8, LANES), F32)
     second = jnp.zeros((8, LANES), F32)
     for axis in range(3):
         taken = jnp.where(hit, take_lanes(solved_ref[axis], low), 0.0)
-        first = first + jac_a[axis:axis + 1] * taken
-        second = second + jac_b[axis:axis + 1] * taken
+        first = first + jac[axis:axis + 1] * taken
+        second = second + jac[axis + 4:axis + 5] * taken
     return jnp.sum(first, axis=0, keepdims=True), jnp.sum(second, axis=0, keepdims=True)
+
+
+def two_level(jac, first, second):
+    both = jac * jnp.where(iota(jac.shape, 0) < 4, first, second)
+    return both + pltpu.roll(both, 4, 0)
+
+
+def kept_rows(solved_ref, index_ref, jac_ref, along_ref, start, chunk):
+    kept_a, kept_b = [], []
+    for tile in range(chunk // LANES):
+        spot = slice(start + tile * LANES, start + (tile + 1) * LANES)
+        first, second = point_spread(solved_ref, index_ref[0:1, spot], index_ref[1:2, spot], jac_ref[:, spot])
+        kept_a.append(along_ref[0:1, spot] - first)
+        kept_b.append(along_ref[1:2, spot] - second)
+    return jnp.concatenate(kept_a, axis=1), jnp.concatenate(kept_b, axis=1)
 
 
 def solve_points(inverse_ref, totals, solved_ref):
@@ -150,11 +192,13 @@
     return total
 
 
-def start_kernel(chunk, count_ref, cam_hbm, pt_hbm, err_hbm, point_hbm, slot_hbm, req_hbm, damp_hbm,
-                 out_ref, camp_ref, pta_ref, ptb_ref, index_ref, inverse_ref,
-                 psum_ref, ssum_ref, solved_ref, cam_ref, pt_ref, err_ref, point_ref, slot_ref, req_ref, damp_ref,
-                 cam_sem, pt_sem, err_sem, point_sem, slot_sem, req_sem, damp_sem):
+def start_kernel(chunk, count_ref, cam_hbm, pt_hbm, err_hbm, point_hbm, slot_hbm, req_hbm, damp_hbm, camdamp_hbm,
+                 out_ref, camp_ref, jac_ref, index_ref, pointhot_ref, slothot_ref, inverse_ref, camdamp_ref,
+                 psum_ref, ssum_ref, solved_ref, pointrows_ref, slotrows_ref,
+                 cam_ref, pt_ref, err_ref, point_ref, slot_ref, req_ref, damp_ref,
+                 cam_sem, pt_sem, err_sem, point_sem, slot_sem, req_sem, damp_sem, camdamp_sem):
     nobs = cam_ref.shape[1]
+    steps = nobs // chunk
     copies = [
         pltpu.make_async_copy(pt_hbm, pt_ref, pt_sem),
         pltpu.make_async_copy(err_hbm, err_ref, err_sem),
@@ -163,20 +207,18 @@
         pltpu.make_async_copy(damp_hbm, damp_ref, damp_sem),
         pltpu.make_async_copy(cam_hbm, cam_ref, cam_sem),
         pltpu.make_async_copy(req_hbm, req_ref, req_sem),
+        pltpu.make_async_copy(camdamp_hbm, camdamp_ref, camdamp_sem),
     ]
     for copy in copies:
         copy.start()
     count = count_ref[0]
-    psum_ref[...] = jnp.zeros_like(psum_ref)
-    ssum_ref[...] = jnp.zeros_like(ssum_ref)
     groups = req_ref.shape[0] * CAP // 256
     for copy in copies[:5]:
         copy.wait()
 
-    def gather_points(step, carry):
-        start = pl.multiple_of(step * chunk, chunk)
-        lanes = pl.ds(start, chunk)
-        live = iota((1, chunk), 1) + start < count
+    def build_points(step):
+        lanes = chunk_lanes(step, chunk)
+        live = iota((1, chunk), 1) + step * chunk < count
         point = point_ref[:, lanes]
         low = point & (LANES - 1)
         group = jnp.where(live, point >> 7, -1)
@@ -185,12 +227,16 @@
         index_ref[1:2, lanes] = group
         index_ref[2:3, lanes] = slot
         index_ref[3:4, lanes] = jnp.where(live, slot >> 8, -1)
+        for tile in range(chunk // LANES):
+            spot = slice(step * chunk + tile * LANES, step * chunk + (tile + 1) * LANES)
+            part = chunk_lanes(tile, LANES)
+            pointhot_ref[spot, :] = one_hot_columns(low[:, part], LANES)
+            slothot_ref[spot, :] = one_hot_columns(slot[:, part] & 255, 256)
         jac = pt_ref[:, lanes]
         zero = jnp.zeros((1, chunk), F32)
+        jac_ref[:, lanes] = jnp.concatenate([jac[0:3], zero, jac[3:6], zero], axis=0)
         jac_a = jnp.concatenate([jac[0:3], zero, jac[0:3], zero], axis=0)
         jac_b = jnp.concatenate([jac[3:6], zero, jac[3:6], zero], axis=0)
-        pta_ref[:, lanes] = jac_a
-        ptb_ref[:, lanes] = jac_b
         turn_a = jnp.concatenate([jac[0:3], zero, jac[1:3], jac[0:1], zero], axis=0)
         turn_b = jnp.concatenate([jac[3:6], zero, jac[4:6], jac[3:4], zero], axis=0)
         err = err_ref[:, lanes]
@@ -198,11 +244,10 @@
         sides = wide_parts(jac_a * err[0:1] + jac_b * err[1:2], 3)
         rows = [block[place:place + 1] for block in blocks for place in (0, 1, 2, 4, 5, 6)]
         rows += [side[place:place + 1] for side in sides for place in (0, 1, 2)]
-        spread = stack_tiles(masked_rows(rows, group_hits(group)))
-        psum_ref[...] += contract(spread, one_hot_rows(low, LANES))
-        return carry
-
-    lax.fori_loop(0, nobs // chunk, gather_points, 0)
+        pointrows_ref[:, lanes] = stack_tiles(masked_rows(rows, group_hits(group)))
+
+    pipelined(steps, build_points, lambda step: add_product(
+        psum_ref, pointrows_ref, pointhot_ref, chunk_lanes(step, chunk), step == 0))
 
     damp = damp_ref[...]
     m00, m11, m22, m01, m12, m20 = [summed_parts(psum_ref, 8 * place, 8, 3, 48) for place in range(6)]
@@ -220,38 +265,27 @@
     for copy in copies[5:]:
         copy.wait()
 
-    def scatter_terms(step, carry):
-        start = pl.multiple_of(step * chunk, chunk)
-        lanes = pl.ds(start, chunk)
-        camp_ref[0:9, lanes] = cam_ref[0:9, lanes]
-        camp_ref[9:16, lanes] = jnp.zeros((7, chunk), F32)
-        camp_ref[16:25, lanes] = cam_ref[9:18, lanes]
-        camp_ref[25:32, lanes] = jnp.zeros((7, chunk), F32)
-        kept_a, kept_b = [], []
-        for tile in range(chunk // LANES):
-            spot = pl.ds(start + tile * LANES, LANES)
-            first, second = point_spread(
-                solved_ref, index_ref[0:1, spot], index_ref[1:2, spot], pta_ref[:, spot], ptb_ref[:, spot])
-            err = err_ref[:, spot]
-            kept_a.append(err[0:1] - first)
-            kept_b.append(err[1:2] - second)
-        kept_a = jnp.concatenate(kept_a, axis=1)
-        kept_b = jnp.concatenate(kept_b, axis=1)
-        cam_a = camp_ref[0:16, lanes]
-        cam_b = camp_ref[16:32, lanes]
+    def build_slots(step):
+        lanes = chunk_lanes(step, chunk)
+        cam_a = cam_ref[0:8, lanes]
+        cam_b = cam_ref[9:17, lanes]
+        last = jnp.concatenate([cam_ref[8:9, lanes], cam_ref[17:18, lanes], jnp.zeros((6, chunk), F32)], axis=0)
+        camp_ref[0:8, lanes] = cam_a
+        camp_ref[8:16, lanes] = cam_b
+        camp_ref[16:24, lanes] = last
+        kept_a, kept_b = kept_rows(solved_ref, index_ref, jac_ref, err_ref, step * chunk, chunk)
         rhs = wide_parts(-(cam_a * kept_a + cam_b * kept_b), 2)
         diag = wide_parts(cam_a * cam_a + cam_b * cam_b, 2)
-        heads = [[part[0:8] for part in rhs], [part[0:8] for part in diag]]
-        tails = [part[8:9] for part in rhs + diag]
-        slot = index_ref[2:3, lanes]
-        spread = spread_slots(heads, tails, index_ref[3:4, lanes], groups)
-        ssum_ref[...] += contract(spread, one_hot_rows(slot & 255, 256))
-        return carry
-
-    lax.fori_loop(0, nobs // chunk, scatter_terms, 0)
+        last_a, last_b = last[0:1], last[1:2]
+        tails = wide_parts(-(last_a * kept_a + last_b * kept_b), 2) + wide_parts(last_a * last_a + last_b * last_b, 2)
+        slotrows_ref[:, lanes] = spread_slots([rhs, diag], tails, index_ref[3:4, lanes], groups)
+
+    pipelined(steps, build_slots, lambda step: add_product(
+        ssum_ref, slotrows_ref, slothot_ref, chunk_lanes(step, chunk), step == 0))
     wanted = req_ref[...].astype(F32)
     wanted = jnp.concatenate([wanted, jnp.zeros_like(wanted)], axis=1)
     left = left_half()
+    left_one = left_half(1)
     for group in range(groups):
         rhs = summed_parts(ssum_ref, 32 * group, 8, 2, 8)
         diag = summed_parts(ssum_ref, 32 * group + 16, 8, 2, 8)
@@ -263,7 +297,6 @@
             row = 20 * (2 * group + half)
             out_ref[row:row + 8] = jnp.where(left, rhs[:, lanes], swap_halves(diag[:, lanes]))
             out_ref[row + 10:row + 18] = jnp.where(left, swap_halves(rhs[:, lanes]), diag[:, lanes])
-            left_one = left_half(1)
             out_ref[row + 8:row + 9] = jnp.where(left_one, rhs_last[:, lanes], swap_halves(diag_last[:, lanes]))
             out_ref[row + 18:row + 19] = jnp.where(left_one, swap_halves(rhs_last[:, lanes]), diag_last[:, lanes])
             owner = 4 * group + 2 * half
@@ -273,15 +306,15 @@
 
 def apply_kernel(chunk, first, *refs):
     if first:
-        (in_ref, camp_ref, pta_ref, ptb_ref, index_ref, inverse_ref, damp_ref, precond_ref,
-         out_ref, table_ref, last_ref, rz_ref, psum_ref, ssum_ref, solved_ref, along_ref) = refs
+        (in_ref, camp_ref, jac_ref, index_ref, pointhot_ref, slothot_ref, inverse_ref, damp_ref, precond_ref,
+         out_ref, table_ref, last_ref, rz_ref, *work) = refs
     else:
-        (in_ref, camp_ref, pta_ref, ptb_ref, index_ref, inverse_ref, damp_ref, precond_ref,
+        (in_ref, camp_ref, jac_ref, index_ref, pointhot_ref, slothot_ref, inverse_ref, damp_ref, precond_ref,
          oldtable_ref, oldlast_ref, oldrz_ref, oldown_ref,
-         out_ref, own_ref, rz_ref, psum_ref, ssum_ref, solved_ref, along_ref, table_ref, last_ref) = refs
+         out_ref, own_ref, rz_ref, *work, table_ref, last_ref) = refs
+    psum_ref, ssum_ref, solved_ref, along_ref, pointrows_ref, slotrows_ref = work
     nobs = camp_ref.shape[1]
-    psum_ref[...] = jnp.zeros_like(psum_ref)
-    ssum_ref[...] = jnp.zeros_like(ssum_ref)
+    steps = nobs // chunk
     pairs = table_ref.shape[0]
     groups = pairs // 2
     rz = carried_scalar(in_ref)
@@ -299,11 +332,10 @@
         table_ref[pair] = head
         last_ref[pair:pair + 1] = tail
 
-    def gather_points(step, carry):
-        start = pl.multiple_of(step * chunk, chunk)
-        lanes = pl.ds(start, chunk)
+    def build_points(step):
+        lanes = chunk_lanes(step, chunk)
         for tile in range(chunk // LANES):
-            spot = pl.ds(start + tile * LANES, LANES)
+            spot = slice(step * chunk + tile * LANES, step * chunk + (tile + 1) * LANES)
             slot = index_ref[2:3, spot]
             low = jnp.broadcast_to(slot & (LANES - 1), (8, LANES))
             high = jnp.broadcast_to(slot >> 7, (8, LANES))
@@ -315,37 +347,32 @@
                 hit = high == iota((8, LANES), 0) + base
                 tail = jnp.where(hit, take_lanes(last_ref[base:base + 8], low), tail)
             tail = jnp.sum(tail, axis=0, keepdims=True)
-            along_ref[0:1, spot] = jnp.sum(camp_ref[0:8, spot] * taken, axis=0, keepdims=True) + camp_ref[8:9, spot] * tail
-            along_ref[1:2, spot] = jnp.sum(camp_ref[16:24, spot] * taken, axis=0, keepdims=True) + camp_ref[24:25, spot] * tail
-        sides = wide_parts(pta_ref[:, lanes] * along_ref[0:1, lanes] + ptb_ref[:, lanes] * along_ref[1:2, lanes], 3)
+            along_ref[0:1, spot] = jnp.sum(camp_ref[0:8, spot] * taken, axis=0, keepdims=True) + camp_ref[16:17, spot] * tail
+            along_ref[1:2, spot] = jnp.sum(camp_ref[8:16, spot] * taken, axis=0, keepdims=True) + camp_ref[17:18, spot] * tail
+        sides = wide_parts(two_level(jac_ref[:, lanes], along_ref[0:1, lanes], along_ref[1:2, lanes]), 3)
         rows = [side[place:place + 1] for side in sides for place in (0, 1, 2)]
-        spread = stack_tiles(masked_rows(rows, group_hits(index_ref[1:2, lanes])))
-        psum_ref[...] += contract(spread, one_hot_rows(index_ref[0:1, lanes], LANES))
-        return carry
-
-    lax.fori_loop(0, nobs // chunk, gather_points, 0)
+        pointrows_ref[:, lanes] = stack_tiles(masked_rows(rows, group_hits(index_ref[1:2, lanes])))
+
+    pipelined(steps, build_points, lambda step: add_product(
+        psum_ref, pointrows_ref, pointhot_ref, chunk_lanes(step, chunk), step == 0))
     solve_points(inverse_ref, [summed_parts(psum_ref, 8 * place, 8, 3, 24) for place in range(3)], solved_ref)
-
-    def scatter_terms(step, carry):
-        start = pl.multiple_of(step * chunk, chunk)
-        lanes = pl.ds(start, chunk)
-        kept_a, kept_b = [], []
-        for tile in range(chunk // LANES):
-            spot = pl.ds(start + tile * LANES, LANES)
-            first_sum, second_sum = point_spread(
-                solved_ref, index_ref[0:1, spot], index_ref[1:2, spot], pta_ref[:, spot], ptb_ref[:, spot])
-            kept_a.append(along_ref[0:1, spot] - first_sum)
-            kept_b.append(along_ref[1:2, spot] - second_sum)
-        kept_a = jnp.concatenate(kept_a, axis=1)
-        kept_b = jnp.concatenate(kept_b, axis=1)
-        terms = wide_parts(camp_ref[0:16, lanes] * kept_a + camp_ref[16:32, lanes] * kept_b, 2)
+    energies = []
+
+    def build_slots(step):
+        lanes = chunk_lanes(step, chunk)
+        kept_a, kept_b = kept_rows(solved_ref, index_ref, jac_ref, along_ref, step * chunk, chunk)
+        heads = wide_parts(camp_ref[0:8, lanes] * kept_a + camp_ref[8:16, lanes] * kept_b, 2)
+        tails = wide_parts(camp_ref[16:17, lanes] * kept_a + camp_ref[17:18, lanes] * kept_b, 2)
         group = index_ref[3:4, lanes]
-        spread = spread_slots([[part[0:8] for part in terms]], [part[8:9] for part in terms], group, groups)
-        ssum_ref[...] += contract(spread, one_hot_rows(index_ref[2:3, lanes] & 255, 256))
+        slotrows_ref[:, lanes] = spread_slots([heads], tails, group, groups)
         energy = along_ref[0:1, lanes] * kept_a + along_ref[1:2, lanes] * kept_b
-        return carry + jnp.where(group >= 0, energy, 0.0)
-
-    energy = lax.fori_loop(0, nobs // chunk, scatter_terms, jnp.zeros((1, chunk), F32))
+        energies.append(jnp.where(group >= 0, energy, 0.0))
+
+    pipelined(steps, build_slots, lambda step: add_product(
+        ssum_ref, slotrows_ref, slothot_ref, chunk_lanes(step, chunk), step == 0))
+    energy = energies[0]
+    for more in energies[1:]:
+        energy = energy + more
     partial = sum_all(energy) + sum_all(damp_ref[...] * own * own)
     for group in range(groups):
         head = summed_parts(ssum_ref, 16 * group, 8, 2, 8)
@@ -473,18 +500,23 @@
     return moved.reshape(blocks.shape)
 
 
+def product_scratch(point_rows, slot_rows, nobs):
+    return [pltpu.VMEM((rows, nobs), BF16) for rows in (point_rows, slot_rows)]
+
+
 def start_call(chunk, *args):
-    _, jac_cam, _, _, _, _, request, _ = args
+    jac_cam, request, cam_damp = args[1], args[6], args[8]
     nobs = jac_cam.shape[1]
     shards = request.shape[0]
     groups = shards * CAP // 256
     copied = args[1:]
-    scratch = [pltpu.VMEM((224, LANES), F32), pltpu.VMEM((groups * 32 + (groups + 7) // 8 * 32, 256), F32),
-               pltpu.VMEM((3, 8, LANES), F32)]
-    scratch += [pltpu.VMEM(arg.shape, arg.dtype) for arg in copied]
+    rows = groups * 32 + (groups + 7) // 8 * 32
+    scratch = [pltpu.VMEM((224, LANES), F32), pltpu.VMEM((rows, 256), F32), pltpu.VMEM((3, 8, LANES), F32)]
+    scratch += product_scratch(224, rows, nobs)
+    scratch += [pltpu.VMEM(arg.shape, arg.dtype) for arg in copied[:-1]]
     scratch += [pltpu.SemaphoreType.DMA] * len(copied)
-    outs = [((shards * 10, LANES), F32), ((32, nobs), F32), ((8, nobs), F32), ((8, nobs), F32),
-            ((8, nobs), jnp.int32), ((6, 8, LANES), F32)]
+    outs = [((shards * 10, LANES), F32), ((24, nobs), F32), ((8, nobs), F32), ((8, nobs), jnp.int32),
+            ((nobs, LANES), BF16), ((nobs, 256), BF16), ((6, 8, LANES), F32), (cam_damp.shape, F32)]
     copied = [pltpu.with_memory_space_constraint(arg, pltpu.HBM) for arg in copied]
     return call(functools.partial(start_kernel, chunk), outs, scratch, args[0], *copied, smem=1, hbm=len(copied))
 
@@ -495,9 +527,11 @@
     shards = arrived.shape[0] // 5
     pairs = shards // 2
     groups = shards // 4
-    cameras = args[6].shape[1]
-    scratch = [pltpu.VMEM((80, LANES), F32), pltpu.VMEM((groups * 16 + (groups + 7) // 8 * 16, 256), F32),
-               pltpu.VMEM((3, 8, LANES), F32), pltpu.VMEM((8, nobs), F32)]
+    cameras = args[7].shape[1]
+    rows = groups * 16 + (groups + 7) // 8 * 16
+    scratch = [pltpu.VMEM((80, LANES), F32), pltpu.VMEM((rows, 256), F32), pltpu.VMEM((3, 8, LANES), F32),
+               pltpu.VMEM((8, nobs), F32)]
+    scratch += product_scratch(80, rows, nobs)
     table = (pairs, 8, LANES)
     last = ((pairs + 7) // 8 * 8, LANES)
     scalar = ((8, LANES), F32)
@@ -515,29 +549,29 @@
     shards = request.shape[0]
     cameras = cam_damp.shape[1]
     slots = shards * CAP
-    chunk = 4096
+    chunk = 1024
     own = ((9, cameras), F32)
     sent = ((shards * 5, LANES), F32)
-    sums, camp, pta, ptb, index, inverse = start_call(
+    sums, camp, jac, index, pointhot, slothot, inverse, damp = start_call(
         chunk, obs_count, jac_cam, jac_pt, obs_residual, obs_point.reshape(1, nobs), obs_slot.reshape(1, nobs),
-        request, pt_damp.reshape(8, LANES))
+        request, pt_damp.reshape(8, LANES), cam_damp)
     arrived = exchange(sums, shards)
     send, residual, scaling, precond, ids = call(
-        owner_start_kernel, [sent, own, own, own, ((1, slots), jnp.int32)], [], arrived, cam_damp)
+        owner_start_kernel, [sent, own, own, own, ((1, slots), jnp.int32)], [], arrived, damp)
     arrived = exchange(send, shards)
     send, table, last, rz = apply_call(
-        chunk, True, arrived, camp, pta, ptb, index, inverse, cam_damp, precond)
+        chunk, True, arrived, camp, jac, index, pointhot, slothot, inverse, damp, precond)
     arrived = exchange(send, shards)
     direction = precond
     send, update, residual, precond = call(
         owner_middle_kernel, [sent, own, own, own], [],
-        arrived, ids, rz, cam_damp, direction, residual, scaling)
+        arrived, ids, rz, damp, direction, residual, scaling)
     arrived = exchange(send, shards)
     send, direction, rz = apply_call(
-        chunk, False, arrived, camp, pta, ptb, index, inverse, cam_damp, precond, table, last, rz, direction)
+        chunk, False, arrived, camp, jac, index, pointhot, slothot, inverse, damp, precond, table, last, rz, direction)
     arrived = exchange(send, shards)
     update, residual = call(
-        owner_end_kernel, [own, own], [], arrived, ids, rz, cam_damp, direction, residual, update)
+        owner_end_kernel, [own, own], [], arrived, ids, rz, damp, direction, residual, update)
     return update, residual
 
 

time: 74.4 us -> 70.9 us (0.953)
  Pallas kernels: 19.1 us -> 15.6 us
    pallas_call x6, Pallas kernels: 19.1 us -> 15.6 us  [call(): pl.pallas_call(kernel, out_shape=[jax.ShapeDtypeStruct(shape, dtype) for...]
where the time goes in v3:
time: 70.9 us; the launch traced here: 70.6 us
  blocking collectives  53.7 us (76%)
  Pallas kernels  15.6 us (22%)
  between operations  1.31 us (2%)
    all_to_all x5, blocking collectives, exchange(): lax.all_to_all(blocks.reshape(shards, 1, -1), AXES, split_axis=0, concat_...  53.7 us
    pallas_call x6, Pallas kernels, call(): pl.pallas_call(kernel, out_shape=[jax.ShapeDtypeStruct(shape, dtype) for...  15.6 us

profile of v3, /device:TPU:0, one launch (start us, length us, event | category | flops | bytes accessed | tf_op | source)
XLA Modules:
  0.0 70.6 jit_solution(1306068155997935721)
XLA Ops:
  1.3 5.0 %shard_map.104 = (f32[320,128]{1,0:T(8,128)S(1)}, f32[24,8192]{1,0:T(8,128)S(1)}, f32[8,8192]{1,0:T(8,128)S(1)}, s32[8,8192]{1,0:T(8,128)S(1)}, bf16[8192,128]{1...) custom-call(s32[1]{0:T(128)S(6)} %copy.16.count_ref, ...), custom_call_target="tpu_custom_call" | custom-call | tf_op jit(solution)/shard_map/pallas_call | solution.py:488
  6.3 16.0 %all_to_all.25 = f32[32,1,1280]{2,1,0:T(1,128)S(1)} all-to-all(f32[32,1,1280]{2,1,0:T(1,128)S(1)} %bitcast.18), channel_id=1, replica_groups=mesh['cell'=8,'img'=4] {'cell','img'}, dimensions={0} | all-to-all | bytes 327680 | tf_op jit(solution)/shard_map/all_to_all | solution.py:499
  22.2 1.1 %shard_map.105 = (f32[160,128]{1,0:T(8,128)S(1)}, f32[9,768]{1,0:T(8,128)S(1)}, f32[9,768]{1,0:T(8,128)S(1)}, f32[9,768]{1,0:T(8,128)S(1)}, s32[1,2048]{1,0:T(1,128)S(1)}) custom-call(f32[320,128]{1,0:T(8,128)S(1)} %bitcast.13, f32[9,768]{1,0:T(8,128)S(1)} %get-tuple-element.27.damp_ref.refs_7_), custom_call_target="tpu_custom_call" | custom-call | tf_op jit(solution)/shard_map/pallas_call | solution.py:488
  23.4 9.5 %all_to_all.26 = f32[32,1,640]{2,1,0:T(1,128)S(1)} all-to-all(f32[32,1,640]{2,1,0:T(1,128)S(1)} %bitcast.21), channel_id=1, replica_groups=mesh['cell'=8,'img'=4] {'cell','img'}, dimensions={0} | all-to-all | bytes 163840 | tf_op jit(solution)/shard_map/all_to_all | solution.py:499
  32.8 3.7 %shard_map.106 = (f32[160,128]{1,0:T(8,128)S(1)}, f32[16,8,128]{2,1,0:T(8,128)S(1)}, f32[16,128]{1,0:T(8,128)S(1)}, f32[8,128]{1,0:T(8,128)S(1)}) custom-call(f32[160,128]{1,0:T(8,128)S(1)} %bitcast.15, f32[24,8192]{1,0:T(8,128)S(1)} %get-tuple-element.29.refs_1_, f32[8,8192]{1,0:T(8,128)S(1)} %get-tuple-element.30.refs_2_, ...), custom_call_target="tpu_custom_call" | custom-call | tf_op jit(solution)/shard_map/pallas_call | solution.py:488
  36.5 9.4 %all_to_all.27 = f32[32,1,640]{2,1,0:T(1,128)S(1)} all-to-all(f32[32,1,640]{2,1,0:T(1,128)S(1)} %bitcast.22), channel_id=1, replica_groups=mesh['cell'=8,'img'=4] {'cell','img'}, dimensions={0} | all-to-all | bytes 163840 | tf_op jit(solution)/shard_map/all_to_all | solution.py:499
  46.0 1.0 %shard_map.107 = (f32[160,128]{1,0:T(8,128)S(1)}, f32[9,768]{1,0:T(8,128)S(1)}, f32[9,768]{1,0:T(8,128)S(1)}, f32[9,768]{1,0:T(8,128)S(1)}) custom-call(f32[160,128]{1,0:T(8,128)S(1)} %bitcast.17, s32[1,2048]{1,0:T(1,128)S(1)} %get-tuple-element.37.ids_ref, f32[8,128]{1,0:T(8,128)S(1)} %get-tuple-element.38.rz_ref.refs_11_, ...), custom_call_target="tpu_custom_call" | custom-call | tf_op jit(solution)/shard_map/pallas_call | solution.py:488
  47.0 9.4 %all_to_all.28 = f32[32,1,640]{2,1,0:T(1,128)S(1)} all-to-all(f32[32,1,640]{2,1,0:T(1,128)S(1)} %bitcast.20), channel_id=1, replica_groups=mesh['cell'=8,'img'=4] {'cell','img'}, dimensions={0} | all-to-all | bytes 163840 | tf_op jit(solution)/shard_map/all_to_all | solution.py:499
  56.4 3.7 %shard_map.108 = (f32[160,128]{1,0:T(8,128)S(1)}, f32[9,768]{1,0:T(8,128)S(1)}, f32[8,128]{1,0:T(8,128)S(1)}) custom-call(f32[160,128]{1,0:T(8,128)S(1)} %bitcast.14, f32[24,8192]{1,0:T(8,128)S(1)} %get-tuple-element.29.refs_1_, f32[8,8192]{1,0:T(8,128)S(1)} %get-tuple-element.30.refs_2_, s32[8,8192]{1,0:T(8,128)S(1)} %get-tuple-element.31.refs_3_, ...), custom_call_target="tpu_custom_call" | custom-call | tf_op jit(solution)/shard_map/pallas_call | solution.py:488
  60.1 9.4 %all_to_all.29 = f32[32,1,640]{2,1,0:T(1,128)S(1)} all-to-all(f32[32,1,640]{2,1,0:T(1,128)S(1)} %bitcast.19), channel_id=1, replica_groups=mesh['cell'=8,'img'=4] {'cell','img'}, dimensions={0} | all-to-all | bytes 163840 | tf_op jit(solution)/shard_map/all_to_all | solution.py:499
  69.5 1.1 %shard_map.109 = (f32[9,768]{1,0:T(8,128)}, f32[9,768]{1,0:T(8,128)}) custom-call(f32[160,128]{1,0:T(8,128)S(1)} %bitcast.16, s32[1,2048]{1,0:T(1,128)S(1)} %get-tuple-element.37.ids_ref, f32[8,128]{1,0:T(8,128)S(1)} %get-tuple-element.46.rz_ref, f32[9,768]{1,0:T(8,128)S(1)} %get-tuple-element.27.damp_ref.refs_7_, ...), custom_call_target="tpu_custom_call" | custom-call | tf_op jit(solution)/shard_map/pallas_call | solution.py:488

commit v4 on v3

--- a/solution.py
+++ b/solution.py
@@ -200,10 +200,10 @@
     nobs = cam_ref.shape[1]
     steps = nobs // chunk
     copies = [
+        pltpu.make_async_copy(point_hbm, point_ref, point_sem),
+        pltpu.make_async_copy(slot_hbm, slot_ref, slot_sem),
         pltpu.make_async_copy(pt_hbm, pt_ref, pt_sem),
         pltpu.make_async_copy(err_hbm, err_ref, err_sem),
-        pltpu.make_async_copy(point_hbm, point_ref, point_sem),
-        pltpu.make_async_copy(slot_hbm, slot_ref, slot_sem),
         pltpu.make_async_copy(damp_hbm, damp_ref, damp_sem),
         pltpu.make_async_copy(cam_hbm, cam_ref, cam_sem),
         pltpu.make_async_copy(req_hbm, req_ref, req_sem),
@@ -213,10 +213,10 @@
         copy.start()
     count = count_ref[0]
     groups = req_ref.shape[0] * CAP // 256
-    for copy in copies[:5]:
+    for copy in copies[:2]:
         copy.wait()
 
-    def build_points(step):
+    for step in range(steps):
         lanes = chunk_lanes(step, chunk)
         live = iota((1, chunk), 1) + step * chunk < count
         point = point_ref[:, lanes]
@@ -232,6 +232,12 @@
             part = chunk_lanes(tile, LANES)
             pointhot_ref[spot, :] = one_hot_columns(low[:, part], LANES)
             slothot_ref[spot, :] = one_hot_columns(slot[:, part] & 255, 256)
+    for copy in copies[2:5]:
+        copy.wait()
+
+    def build_points(step):
+        lanes = chunk_lanes(step, chunk)
+        group = index_ref[1:2, lanes]
         jac = pt_ref[:, lanes]
         zero = jnp.zeros((1, chunk), F32)
         jac_ref[:, lanes] = jnp.concatenate([jac[0:3], zero, jac[3:6], zero], axis=0)
@@ -407,19 +413,18 @@
 
 def send_wanted(out_ref, precond, ids, scalar):
     cameras = precond.shape[1]
+    blocks = cameras // LANES
+    spare = [jnp.zeros((1, LANES), F32)] * (8 - blocks)
+    last = jnp.concatenate([precond[8:9, block * LANES:(block + 1) * LANES] for block in range(blocks)] + spare, axis=0)
     for pair in range(out_ref.shape[0] // 10):
         own = ids[:, pair * LANES:(pair + 1) * LANES]
         low = jnp.broadcast_to(own & (LANES - 1), (8, LANES))
         high = jnp.broadcast_to(own >> 7, (8, LANES))
         head = jnp.zeros((8, LANES), F32)
-        tail = jnp.zeros((8, LANES), F32)
-        for block in range(cameras // LANES):
-            lanes = slice(block * LANES, (block + 1) * LANES)
-            hit = high == block
-            head = jnp.where(hit, take_lanes(precond[0:8, lanes], low), head)
-            last = jnp.broadcast_to(precond[8:9, lanes], (8, LANES))
-            tail = jnp.where(hit, take_lanes(last, low), tail)
-        store_five(out_ref, pair, head, tail[0:1], scalar)
+        for block in range(blocks):
+            head = jnp.where(high == block, take_lanes(precond[0:8, block * LANES:(block + 1) * LANES], low), head)
+        tail = jnp.where(high == iota((8, LANES), 0), take_lanes(last, low), 0.0)
+        store_five(out_ref, pair, head, jnp.sum(tail, axis=0, keepdims=True), scalar)
 
 
 def owner_start_kernel(in_ref, damp_ref, out_ref, residual_ref, scaling_ref, precond_ref, ids_ref):
@@ -549,11 +554,11 @@
     shards = request.shape[0]
     cameras = cam_damp.shape[1]
     slots = shards * CAP
-    chunk = 1024
+    start_chunk, chunk = 512, 256
     own = ((9, cameras), F32)
     sent = ((shards * 5, LANES), F32)
     sums, camp, jac, index, pointhot, slothot, inverse, damp = start_call(
-        chunk, obs_count, jac_cam, jac_pt, obs_residual, obs_point.reshape(1, nobs), obs_slot.reshape(1, nobs),
+        start_chunk, obs_count, jac_cam, jac_pt, obs_residual, obs_point.reshape(1, nobs), obs_slot.reshape(1, nobs),
         request, pt_damp.reshape(8, LANES), cam_damp)
     arrived = exchange(sums, shards)
     send, residual, scaling, precond, ids = call(

time: 70.9 us -> 70.2 us (level)
  no operation moved by 1% of the time
where the time goes in v4:
time: 70.2 us; the launch traced here: 69.9 us
  blocking collectives  53.7 us (76%)
  Pallas kernels  14.9 us (21%)
  between operations  1.31 us (2%)
    all_to_all x5, blocking collectives, exchange(): lax.all_to_all(blocks.reshape(shards, 1, -1), AXES, split_axis=0, concat_...  53.7 us
    pallas_call x6, Pallas kernels, call(): pl.pallas_call(kernel, out_shape=[jax.ShapeDtypeStruct(shape, dtype) for...  14.9 us

profile of v4, /device:TPU:0, one launch (start us, length us, event | category | flops | bytes accessed | tf_op | source)
XLA Modules:
  0.0 69.9 jit_solution(17598305038039532821)
XLA Ops:
  1.3 4.8 %shard_map.104 = (f32[320,128]{1,0:T(8,128)S(1)}, f32[24,8192]{1,0:T(8,128)S(1)}, f32[8,8192]{1,0:T(8,128)S(1)}, s32[8,8192]{1,0:T(8,128)S(1)}, bf16[8192,128]{1...) custom-call(s32[1]{0:T(128)S(6)} %copy.16.count_ref, ...), custom_call_target="tpu_custom_call" | custom-call | tf_op jit(solution)/shard_map/pallas_call | solution.py:493
  6.1 16.0 %all_to_all.25 = f32[32,1,1280]{2,1,0:T(1,128)S(1)} all-to-all(f32[32,1,1280]{2,1,0:T(1,128)S(1)} %bitcast.18), channel_id=1, replica_groups=mesh['cell'=8,'img'=4] {'cell','img'}, dimensions={0} | all-to-all | bytes 327680 | tf_op jit(solution)/shard_map/all_to_all | solution.py:504
  22.1 0.9 %shard_map.105 = (f32[160,128]{1,0:T(8,128)S(1)}, f32[9,768]{1,0:T(8,128)S(1)}, f32[9,768]{1,0:T(8,128)S(1)}, f32[9,768]{1,0:T(8,128)S(1)}, s32[1,2048]{1,0:T(1,128)S(1)}) custom-call(f32[320,128]{1,0:T(8,128)S(1)} %bitcast.13, f32[9,768]{1,0:T(8,128)S(1)} %get-tuple-element.27.damp_ref.refs_7_), custom_call_target="tpu_custom_call" | custom-call | tf_op jit(solution)/shard_map/pallas_call | solution.py:493
  23.0 9.5 %all_to_all.26 = f32[32,1,640]{2,1,0:T(1,128)S(1)} all-to-all(f32[32,1,640]{2,1,0:T(1,128)S(1)} %bitcast.21), channel_id=1, replica_groups=mesh['cell'=8,'img'=4] {'cell','img'}, dimensions={0} | all-to-all | bytes 163840 | tf_op jit(solution)/shard_map/all_to_all | solution.py:504
  32.5 3.6 %shard_map.106 = (f32[160,128]{1,0:T(8,128)S(1)}, f32[16,8,128]{2,1,0:T(8,128)S(1)}, f32[16,128]{1,0:T(8,128)S(1)}, f32[8,128]{1,0:T(8,128)S(1)}) custom-call(f32[160,128]{1,0:T(8,128)S(1)} %bitcast.15, f32[24,8192]{1,0:T(8,128)S(1)} %get-tuple-element.29.refs_1_, f32[8,8192]{1,0:T(8,128)S(1)} %get-tuple-element.30.refs_2_, ...), custom_call_target="tpu_custom_call" | custom-call | tf_op jit(solution)/shard_map/pallas_call | solution.py:493
  36.1 9.4 %all_to_all.27 = f32[32,1,640]{2,1,0:T(1,128)S(1)} all-to-all(f32[32,1,640]{2,1,0:T(1,128)S(1)} %bitcast.22), channel_id=1, replica_groups=mesh['cell'=8,'img'=4] {'cell','img'}, dimensions={0} | all-to-all | bytes 163840 | tf_op jit(solution)/shard_map/all_to_all | solution.py:504
  45.5 0.9 %shard_map.107 = (f32[160,128]{1,0:T(8,128)S(1)}, f32[9,768]{1,0:T(8,128)S(1)}, f32[9,768]{1,0:T(8,128)S(1)}, f32[9,768]{1,0:T(8,128)S(1)}) custom-call(f32[160,128]{1,0:T(8,128)S(1)} %bitcast.17, s32[1,2048]{1,0:T(1,128)S(1)} %get-tuple-element.37.ids_ref, f32[8,128]{1,0:T(8,128)S(1)} %get-tuple-element.38.rz_ref.refs_11_, ...), custom_call_target="tpu_custom_call" | custom-call | tf_op jit(solution)/shard_map/pallas_call | solution.py:493
  46.4 9.4 %all_to_all.28 = f32[32,1,640]{2,1,0:T(1,128)S(1)} all-to-all(f32[32,1,640]{2,1,0:T(1,128)S(1)} %bitcast.20), channel_id=1, replica_groups=mesh['cell'=8,'img'=4] {'cell','img'}, dimensions={0} | all-to-all | bytes 163840 | tf_op jit(solution)/shard_map/all_to_all | solution.py:504
  55.8 3.6 %shard_map.108 = (f32[160,128]{1,0:T(8,128)S(1)}, f32[9,768]{1,0:T(8,128)S(1)}, f32[8,128]{1,0:T(8,128)S(1)}) custom-call(f32[160,128]{1,0:T(8,128)S(1)} %bitcast.14, f32[24,8192]{1,0:T(8,128)S(1)} %get-tuple-element.29.refs_1_, f32[8,8192]{1,0:T(8,128)S(1)} %get-tuple-element.30.refs_2_, s32[8,8192]{1,0:T(8,128)S(1)} %get-tuple-element.31.refs_3_, ...), custom_call_target="tpu_custom_call" | custom-call | tf_op jit(solution)/shard_map/pallas_call | solution.py:493
  59.4 9.4 %all_to_all.29 = f32[32,1,640]{2,1,0:T(1,128)S(1)} all-to-all(f32[32,1,640]{2,1,0:T(1,128)S(1)} %bitcast.19), channel_id=1, replica_groups=mesh['cell'=8,'img'=4] {'cell','img'}, dimensions={0} | all-to-all | bytes 163840 | tf_op jit(solution)/shard_map/all_to_all | solution.py:504
  68.8 1.1 %shard_map.109 = (f32[9,768]{1,0:T(8,128)}, f32[9,768]{1,0:T(8,128)}) custom-call(f32[160,128]{1,0:T(8,128)S(1)} %bitcast.16, s32[1,2048]{1,0:T(1,128)S(1)} %get-tuple-element.37.ids_ref, f32[8,128]{1,0:T(8,128)S(1)} %get-tuple-element.46.rz_ref, f32[9,768]{1,0:T(8,128)S(1)} %get-tuple-element.27.damp_ref.refs_7_, ...), custom_call_target="tpu_custom_call" | custom-call | tf_op jit(solution)/shard_map/pallas_call | solution.py:493

commit v5 on v4

--- a/solution.py
+++ b/solution.py
@@ -21,6 +21,21 @@
 
 def take_lanes(table, lanes):
     return jnp.take_along_axis(table, lanes, axis=1, mode="promise_in_bounds")
+
+
+def take_tables(tables, low, high):
+    bits = (len(tables) - 1).bit_length()
+    hits = [(high & (1 << bit)) != 0 for bit in range(bits)]
+
+    def pick(base, bit):
+        if bit < 0:
+            return take_lanes(tables[base](), low)
+        other = base + (1 << bit)
+        if other >= len(tables):
+            return pick(base, bit - 1)
+        return jnp.where(hits[bit], pick(other, bit - 1), pick(base, bit - 1))
+
+    return pick(0, bits - 1)
 
 
 def contract(left, right):
@@ -345,9 +360,7 @@
             slot = index_ref[2:3, spot]
             low = jnp.broadcast_to(slot & (LANES - 1), (8, LANES))
             high = jnp.broadcast_to(slot >> 7, (8, LANES))
-            taken = jnp.zeros((8, LANES), F32)
-            for pair in range(pairs):
-                taken = jnp.where(high == pair, take_lanes(table_ref[pair], low), taken)
+            taken = take_tables([functools.partial(table_ref.__getitem__, pair) for pair in range(pairs)], low, high)
             tail = jnp.zeros((8, LANES), F32)
             for base in range(0, pairs, 8):
                 hit = high == iota((8, LANES), 0) + base
@@ -420,9 +433,9 @@
         own = ids[:, pair * LANES:(pair + 1) * LANES]
         low = jnp.broadcast_to(own & (LANES - 1), (8, LANES))
         high = jnp.broadcast_to(own >> 7, (8, LANES))
-        head = jnp.zeros((8, LANES), F32)
-        for block in range(blocks):
-            head = jnp.where(high == block, take_lanes(precond[0:8, block * LANES:(block + 1) * LANES], low), head)
+        head = take_tables(
+            [functools.partial(lambda start: precond[0:8, start:start + LANES], block * LANES) for block in range(blocks)],
+            low, high)
         tail = jnp.where(high == iota((8, LANES), 0), take_lanes(last, low), 0.0)
         store_five(out_ref, pair, head, jnp.sum(tail, axis=0, keepdims=True), scalar)
 

time: 70.2 us -> 69.6 us (level)
  no operation moved by 1% of the time
where the time goes in v5:
time: 69.6 us; the launch traced here: 69.3 us
  blocking collectives  53.7 us (77%)
  Pallas kernels  14.3 us (21%)
  between operations  1.32 us (2%)
    all_to_all x5, blocking collectives, exchange(): lax.all_to_all(blocks.reshape(shards, 1, -1), AXES, split_axis=0, concat_...  53.7 us
    pallas_call x6, Pallas kernels, call(): pl.pallas_call(kernel, out_shape=[jax.ShapeDtypeStruct(shape, dtype) for...  14.3 us

profile of v5, /device:TPU:0, one launch (start us, length us, event | category | flops | bytes accessed | tf_op | source)
XLA Modules:
  0.0 69.3 jit_solution(8190557859641681311)
XLA Ops:
  1.3 4.8 %shard_map.104 = (f32[320,128]{1,0:T(8,128)S(1)}, f32[24,8192]{1,0:T(8,128)S(1)}, f32[8,8192]{1,0:T(8,128)S(1)}, s32[8,8192]{1,0:T(8,128)S(1)}, bf16[8192,128]{1...) custom-call(s32[1]{0:T(128)S(6)} %copy.16.count_ref, ...), custom_call_target="tpu_custom_call" | custom-call | tf_op jit(solution)/shard_map/pallas_call | solution.py:506
  6.1 16.0 %all_to_all.25 = f32[32,1,1280]{2,1,0:T(1,128)S(1)} all-to-all(f32[32,1,1280]{2,1,0:T(1,128)S(1)} %bitcast.18), channel_id=1, replica_groups=mesh['cell'=8,'img'=4] {'cell','img'}, dimensions={0} | all-to-all | bytes 327680 | tf_op jit(solution)/shard_map/all_to_all | solution.py:517
  22.1 0.9 %shard_map.105 = (f32[160,128]{1,0:T(8,128)S(1)}, f32[9,768]{1,0:T(8,128)S(1)}, f32[9,768]{1,0:T(8,128)S(1)}, f32[9,768]{1,0:T(8,128)S(1)}, s32[1,2048]{1,0:T(1,128)S(1)}) custom-call(f32[320,128]{1,0:T(8,128)S(1)} %bitcast.13, f32[9,768]{1,0:T(8,128)S(1)} %get-tuple-element.27.damp_ref.refs_7_), custom_call_target="tpu_custom_call" | custom-call | tf_op jit(solution)/shard_map/pallas_call | solution.py:506
  23.0 9.5 %all_to_all.26 = f32[32,1,640]{2,1,0:T(1,128)S(1)} all-to-all(f32[32,1,640]{2,1,0:T(1,128)S(1)} %bitcast.21), channel_id=1, replica_groups=mesh['cell'=8,'img'=4] {'cell','img'}, dimensions={0} | all-to-all | bytes 163840 | tf_op jit(solution)/shard_map/all_to_all | solution.py:517
  32.5 3.3 %shard_map.106 = (f32[160,128]{1,0:T(8,128)S(1)}, f32[16,8,128]{2,1,0:T(8,128)S(1)}, f32[16,128]{1,0:T(8,128)S(1)}, f32[8,128]{1,0:T(8,128)S(1)}) custom-call(f32[160,128]{1,0:T(8,128)S(1)} %bitcast.15, f32[24,8192]{1,0:T(8,128)S(1)} %get-tuple-element.29.refs_1_, f32[8,8192]{1,0:T(8,128)S(1)} %get-tuple-element.30.refs_2_, ...), custom_call_target="tpu_custom_call" | custom-call | tf_op jit(solution)/shard_map/pallas_call | solution.py:506
  35.8 9.4 %all_to_all.27 = f32[32,1,640]{2,1,0:T(1,128)S(1)} all-to-all(f32[32,1,640]{2,1,0:T(1,128)S(1)} %bitcast.22), channel_id=1, replica_groups=mesh['cell'=8,'img'=4] {'cell','img'}, dimensions={0} | all-to-all | bytes 163840 | tf_op jit(solution)/shard_map/all_to_all | solution.py:517
  45.2 0.9 %shard_map.107 = (f32[160,128]{1,0:T(8,128)S(1)}, f32[9,768]{1,0:T(8,128)S(1)}, f32[9,768]{1,0:T(8,128)S(1)}, f32[9,768]{1,0:T(8,128)S(1)}) custom-call(f32[160,128]{1,0:T(8,128)S(1)} %bitcast.17, s32[1,2048]{1,0:T(1,128)S(1)} %get-tuple-element.37.ids_ref, f32[8,128]{1,0:T(8,128)S(1)} %get-tuple-element.38.rz_ref.refs_11_, ...), custom_call_target="tpu_custom_call" | custom-call | tf_op jit(solution)/shard_map/pallas_call | solution.py:506
  46.1 9.4 %all_to_all.28 = f32[32,1,640]{2,1,0:T(1,128)S(1)} all-to-all(f32[32,1,640]{2,1,0:T(1,128)S(1)} %bitcast.20), channel_id=1, replica_groups=mesh['cell'=8,'img'=4] {'cell','img'}, dimensions={0} | all-to-all | bytes 163840 | tf_op jit(solution)/shard_map/all_to_all | solution.py:517
  55.5 3.3 %shard_map.108 = (f32[160,128]{1,0:T(8,128)S(1)}, f32[9,768]{1,0:T(8,128)S(1)}, f32[8,128]{1,0:T(8,128)S(1)}) custom-call(f32[160,128]{1,0:T(8,128)S(1)} %bitcast.14, f32[24,8192]{1,0:T(8,128)S(1)} %get-tuple-element.29.refs_1_, f32[8,8192]{1,0:T(8,128)S(1)} %get-tuple-element.30.refs_2_, s32[8,8192]{1,0:T(8,128)S(1)} %get-tuple-element.31.refs_3_, ...), custom_call_target="tpu_custom_call" | custom-call | tf_op jit(solution)/shard_map/pallas_call | solution.py:506
  58.8 9.4 %all_to_all.29 = f32[32,1,640]{2,1,0:T(1,128)S(1)} all-to-all(f32[32,1,640]{2,1,0:T(1,128)S(1)} %bitcast.19), channel_id=1, replica_groups=mesh['cell'=8,'img'=4] {'cell','img'}, dimensions={0} | all-to-all | bytes 163840 | tf_op jit(solution)/shard_map/all_to_all | solution.py:517
  68.2 1.1 %shard_map.109 = (f32[9,768]{1,0:T(8,128)}, f32[9,768]{1,0:T(8,128)}) custom-call(f32[160,128]{1,0:T(8,128)S(1)} %bitcast.16, s32[1,2048]{1,0:T(1,128)S(1)} %get-tuple-element.37.ids_ref, f32[8,128]{1,0:T(8,128)S(1)} %get-tuple-element.46.rz_ref, f32[9,768]{1,0:T(8,128)S(1)} %get-tuple-element.27.damp_ref.refs_7_, ...), custom_call_target="tpu_custom_call" | custom-call | tf_op jit(solution)/shard_map/pallas_call | solution.py:506

commit v6 on v5

--- a/solution.py
+++ b/solution.py
@@ -145,9 +145,7 @@
 def pipelined(steps, build, product):
     for step in range(steps):
         build(step)
-        if step:
-            product(step - 1)
-    product(steps - 1)
+        product(step)
 
 
 def chunk_lanes(step, chunk):

time: 69.6 us -> 69.6 us (level)
  no operation moved by 1% of the time
where the time goes in v6:
time: 69.6 us; the launch traced here: 69.3 us
  blocking collectives  53.7 us (77%)
  Pallas kernels  14.3 us (21%)
  between operations  1.32 us (2%)
    all_to_all x5, blocking collectives, exchange(): lax.all_to_all(blocks.reshape(shards, 1, -1), AXES, split_axis=0, concat_...  53.7 us
    pallas_call x6, Pallas kernels, call(): pl.pallas_call(kernel, out_shape=[jax.ShapeDtypeStruct(shape, dtype) for...  14.3 us

profile of v6, /device:TPU:0, one launch (start us, length us, event | category | flops | bytes accessed | tf_op | source)
XLA Modules:
  0.0 69.3 jit_solution(8190557859641681311)
XLA Ops:
  1.3 4.8 %shard_map.104 = (f32[320,128]{1,0:T(8,128)S(1)}, f32[24,8192]{1,0:T(8,128)S(1)}, f32[8,8192]{1,0:T(8,128)S(1)}, s32[8,8192]{1,0:T(8,128)S(1)}, bf16[8192,128]{1...) custom-call(s32[1]{0:T(128)S(6)} %copy.16.count_ref, ...), custom_call_target="tpu_custom_call" | custom-call | tf_op jit(solution)/shard_map/pallas_call | solution.py:504
  6.1 16.0 %all_to_all.25 = f32[32,1,1280]{2,1,0:T(1,128)S(1)} all-to-all(f32[32,1,1280]{2,1,0:T(1,128)S(1)} %bitcast.18), channel_id=1, replica_groups=mesh['cell'=8,'img'=4] {'cell','img'}, dimensions={0} | all-to-all | bytes 327680 | tf_op jit(solution)/shard_map/all_to_all | solution.py:515
  22.1 0.9 %shard_map.105 = (f32[160,128]{1,0:T(8,128)S(1)}, f32[9,768]{1,0:T(8,128)S(1)}, f32[9,768]{1,0:T(8,128)S(1)}, f32[9,768]{1,0:T(8,128)S(1)}, s32[1,2048]{1,0:T(1,128)S(1)}) custom-call(f32[320,128]{1,0:T(8,128)S(1)} %bitcast.13, f32[9,768]{1,0:T(8,128)S(1)} %get-tuple-element.27.damp_ref.refs_7_), custom_call_target="tpu_custom_call" | custom-call | tf_op jit(solution)/shard_map/pallas_call | solution.py:504
  23.0 9.5 %all_to_all.26 = f32[32,1,640]{2,1,0:T(1,128)S(1)} all-to-all(f32[32,1,640]{2,1,0:T(1,128)S(1)} %bitcast.21), channel_id=1, replica_groups=mesh['cell'=8,'img'=4] {'cell','img'}, dimensions={0} | all-to-all | bytes 163840 | tf_op jit(solution)/shard_map/all_to_all | solution.py:515
  32.5 3.3 %shard_map.106 = (f32[160,128]{1,0:T(8,128)S(1)}, f32[16,8,128]{2,1,0:T(8,128)S(1)}, f32[16,128]{1,0:T(8,128)S(1)}, f32[8,128]{1,0:T(8,128)S(1)}) custom-call(f32[160,128]{1,0:T(8,128)S(1)} %bitcast.15, f32[24,8192]{1,0:T(8,128)S(1)} %get-tuple-element.29.refs_1_, f32[8,8192]{1,0:T(8,128)S(1)} %get-tuple-element.30.refs_2_, ...), custom_call_target="tpu_custom_call" | custom-call | tf_op jit(solution)/shard_map/pallas_call | solution.py:504
  35.8 9.4 %all_to_all.27 = f32[32,1,640]{2,1,0:T(1,128)S(1)} all-to-all(f32[32,1,640]{2,1,0:T(1,128)S(1)} %bitcast.22), channel_id=1, replica_groups=mesh['cell'=8,'img'=4] {'cell','img'}, dimensions={0} | all-to-all | bytes 163840 | tf_op jit(solution)/shard_map/all_to_all | solution.py:515
  45.2 0.9 %shard_map.107 = (f32[160,128]{1,0:T(8,128)S(1)}, f32[9,768]{1,0:T(8,128)S(1)}, f32[9,768]{1,0:T(8,128)S(1)}, f32[9,768]{1,0:T(8,128)S(1)}) custom-call(f32[160,128]{1,0:T(8,128)S(1)} %bitcast.17, s32[1,2048]{1,0:T(1,128)S(1)} %get-tuple-element.37.ids_ref, f32[8,128]{1,0:T(8,128)S(1)} %get-tuple-element.38.rz_ref.refs_11_, ...), custom_call_target="tpu_custom_call" | custom-call | tf_op jit(solution)/shard_map/pallas_call | solution.py:504
  46.1 9.4 %all_to_all.28 = f32[32,1,640]{2,1,0:T(1,128)S(1)} all-to-all(f32[32,1,640]{2,1,0:T(1,128)S(1)} %bitcast.20), channel_id=1, replica_groups=mesh['cell'=8,'img'=4] {'cell','img'}, dimensions={0} | all-to-all | bytes 163840 | tf_op jit(solution)/shard_map/all_to_all | solution.py:515
  55.5 3.3 %shard_map.108 = (f32[160,128]{1,0:T(8,128)S(1)}, f32[9,768]{1,0:T(8,128)S(1)}, f32[8,128]{1,0:T(8,128)S(1)}) custom-call(f32[160,128]{1,0:T(8,128)S(1)} %bitcast.14, f32[24,8192]{1,0:T(8,128)S(1)} %get-tuple-element.29.refs_1_, f32[8,8192]{1,0:T(8,128)S(1)} %get-tuple-element.30.refs_2_, s32[8,8192]{1,0:T(8,128)S(1)} %get-tuple-element.31.refs_3_, ...), custom_call_target="tpu_custom_call" | custom-call | tf_op jit(solution)/shard_map/pallas_call | solution.py:504
  58.8 9.4 %all_to_all.29 = f32[32,1,640]{2,1,0:T(1,128)S(1)} all-to-all(f32[32,1,640]{2,1,0:T(1,128)S(1)} %bitcast.19), channel_id=1, replica_groups=mesh['cell'=8,'img'=4] {'cell','img'}, dimensions={0} | all-to-all | bytes 163840 | tf_op jit(solution)/shard_map/all_to_all | solution.py:515
  68.2 1.1 %shard_map.109 = (f32[9,768]{1,0:T(8,128)}, f32[9,768]{1,0:T(8,128)}) custom-call(f32[160,128]{1,0:T(8,128)S(1)} %bitcast.16, s32[1,2048]{1,0:T(1,128)S(1)} %get-tuple-element.37.ids_ref, f32[8,128]{1,0:T(8,128)S(1)} %get-tuple-element.46.rz_ref, f32[9,768]{1,0:T(8,128)S(1)} %get-tuple-element.27.damp_ref.refs_7_, ...), custom_call_target="tpu_custom_call" | custom-call | tf_op jit(solution)/shard_map/pallas_call | solution.py:504
